TPU v7x, 32 devices: a whole 2x2x4 slice. The times are simulated.
32 devices in a mesh: groups: 2 (over x), rows: 16 (over z, y, core).
Axes of the slice: x: 2, y: 2, z: 4, core: 2. Of those that a mesh axis runs over, the one named last changes fastest.
Arguments:
- features: bfloat16 [3, 256, 8192], P(None, ('groups', 'rows')), parts along dimension 1, may hold values from -6 to 6
- carried: bfloat16 [2, 256, 8192], P(None, ('groups', 'rows')), parts along dimension 1, may hold values from -6 to 6
- flow_shift: int32 [3, 32, 2], P(None, ('groups', 'rows')), parts along dimension 1, may hold values from -8 to 8, as said below
- clip_start: int32 [8], P('groups'), parts along dimension 0, may hold values from 0 to 3
- join_weight: bfloat16 [3, 576, 64], replicated, may hold values from -0.15625 to 0.15625
- res_weight: bfloat16 [4, 3, 192, 64], replicated, may hold values from -0.25 to 0.25
Outputs:
- propagated: bfloat16 [3, 256, 8192], P(None, ('groups', 'rows')), parts along dimension 1
There are 2 independent parts, one for each index of `groups`. A program takes and returns all parts, laid end to end along the dimension named above; an argument that names none is the same for every part. Nothing has to cross between parts.
Inputs may be any that keep to these rules, and one draw needn't show every extreme that they name: `flow_shift`: both ends of the range occur in every draw. `clip_start`: 3 means that the owner begins no clip in these steps.
All inputs are finite; a program needn't handle non-finite values.
Results may differ from a plain program's by a relative error of at most 0.014.
Values may be sent and summed in bfloat16 or wider, within the bound.
No kernel may reach another device: no remote copies, remote signals or barrier semaphores. Data moves between devices by JAX's collectives and lax.ppermute only.
A program may use at most 64 MiB of HBM per device.

v0:
```python
import jax
import jax.numpy as jnp
from jax import lax
from jax.experimental import pallas as pl
from jax.experimental.pallas import tpu as pltpu
from jax.sharding import PartitionSpec as P


TICKS = 3
SECTIONS = 4
RES_BLOCKS = 2
RIM = 1 + 2 * RES_BLOCKS
PAD = 8
SUB = 8
GRANT = 24 << 20

BF16 = jnp.bfloat16
F32 = jnp.float32
VMEM = pl.BlockSpec(memory_space=pltpu.VMEM)
SMEM = pl.BlockSpec(memory_space=pltpu.SMEM)
HBM = pl.BlockSpec(memory_space=pltpu.HBM)


def in_hbm(block):
    return pltpu.with_memory_space_constraint(block, pltpu.HBM)


def lane_low(lanes):
    return lax.broadcasted_iota(jnp.int32, (SUB, lanes), 1) < lanes // 2


def sublane(lanes):
    return lax.broadcasted_iota(jnp.int32, (SUB, lanes), 0)


def store_operand(dst, index, groups, low):
    here = jnp.concatenate(groups[1:-1], axis=0)
    beside = jnp.concatenate(
        [jnp.where(low, groups[v + 2], groups[v]) for v in range(len(groups) - 2)], axis=0
    )
    dst[index + (0,)] = here.astype(BF16)
    dst[index + (1,)] = beside.astype(BF16)


def put(dst, index, row, low, sub):
    count = row.shape[0] // SUB
    groups = [row[SUB * v : SUB * v + SUB] for v in range(count)]
    before = jnp.where(sub > 0, pltpu.roll(groups[-1], 1, 0), 0.0)
    after = jnp.where(sub < SUB - 1, pltpu.roll(groups[0], SUB - 1, 0), 0.0)
    store_operand(dst, index, [before] + groups + [after], low)


def stage(padded, row, value, interleaved):
    pairs = value.shape[0]
    count = pairs // SUB
    if interleaved:
        for v in range(count):
            padded[row, pl.ds(PAD + v, SUB, stride=count), :] = value[SUB * v : SUB * v + SUB]
    else:
        padded[row, PAD : PAD + pairs, :] = value


def put_plain(dst, index, padded, row, low):
    count = (padded.shape[1] - 2 * PAD) // SUB
    groups = [
        padded[row, pl.ds(PAD + v, SUB, stride=count), :] for v in range(-1, count + 1)
    ]
    store_operand(dst, index, groups, low)


def put_warped(dst, index, padded, row, shift, low, sub):
    count = (padded.shape[1] - 2 * PAD) // SUB
    lanes = padded.shape[2]
    start = PAD - (shift >> 1)
    is_odd = (shift & 1) == 1
    raw = [
        padded[row, pl.ds(start + v, SUB, stride=count), :] for v in range(-2, count + 1)
    ]
    groups = []
    for v in range(1, len(raw)):
        odd = pltpu.roll(jnp.where(low, raw[v], raw[v - 1]), lanes // 2, 1)
        groups.append(jnp.where(is_odd, odd, raw[v]))
    groups[0] = jnp.where(sub > 0, groups[0], 0.0)
    groups[-1] = jnp.where(sub < SUB - 1, groups[-1], 0.0)
    store_operand(dst, index, groups, low)


def two_row_weight(w_ref, layers):
    rows = []
    for layer in layers:
        zero = jnp.zeros(w_ref.shape[2:], BF16)
        w = [w_ref[layer, a] for a in range(3)]
        for pair in ((w[0], zero), (w[1], w[0]), (w[2], w[1]), (zero, w[2])):
            rows.append(jnp.concatenate(pair, axis=1))
    return jnp.concatenate(rows, axis=0)


def two_row_conv(fetches, first, count, w_ref, layers):
    columns = []
    for fetch in fetches:
        for i in range(4):
            for part in range(2):
                columns.append(
                    jnp.concatenate(
                        [fetch(2 * (first + k) + i, part) for k in range(count)], axis=0
                    )
                )
    return jnp.dot(
        jnp.concatenate(columns, axis=1),
        two_row_weight(w_ref, layers),
        preferred_element_type=F32,
    )


def scalars_of(row):
    half = row.shape[0] // 2
    wide = row.astype(F32)
    return (
        jnp.max(wide[0:SUB]).astype(jnp.int32),
        jnp.max(wide[half : half + SUB]).astype(jnp.int32),
    )


def local_span(band_rows):
    return (RIM + 1) // 2, (RIM + band_rows - 4) // 2 + 1


def clear_pads(padded):
    rows, long, lanes = padded.shape
    for row in range(rows):
        padded[row, 0:PAD, :] = jnp.zeros((PAD, lanes), F32)
        padded[row, long - PAD :, :] = jnp.zeros((PAD, lanes), F32)


class Place:
    def __init__(self, index, clip, slots):
        bands = slots // SECTIONS
        position = lax.rem(index[0] + (slots - bands // 2), slots)
        self.band = lax.rem(position, bands)
        self.owner = lax.div(position, bands)
        self.clip = clip
        self.even = lax.rem(self.band, 2) == 0
        self.above = self.band > 0
        self.below = self.band < bands - 1

    def keep(self, tick):
        return self.clip[lax.rem(self.owner + tick, SECTIONS)] != tick


def natural_to_rows(scratch, block):
    rows = block.shape[0]
    lanes = scratch.shape[1]
    pairs = block.shape[1] // lanes
    pitch = scratch.shape[0] // rows
    for p in range(pairs):
        tile = block[:, p * lanes : (p + 1) * lanes].astype(F32)
        scratch[pl.ds(p, rows, stride=pitch), :] = tile
    return [scratch[r * pitch : r * pitch + pairs, :].astype(BF16) for r in range(rows)]


def shift_row(flow, tick, pairs, lanes):
    halves = [
        jnp.full((pairs // 2, lanes), flow[0, which, tick].astype(F32)) for which in range(2)
    ]
    return jnp.concatenate(halves, axis=0).astype(BF16)


def pack_kernel(
    slots, index, flow_in, carried, features, own, first_one, first_two, natural, scratch, sems,
    flow,
):
    _, rows, pairs, lanes = own.shape
    place = Place(index, None, slots)
    copies = [
        pltpu.make_async_copy(block, natural.at[part], sems.at[part])
        for part, block in enumerate((carried.at[0], carried.at[1], features.at[0]))
    ]
    copies.append(pltpu.make_async_copy(flow_in, flow, sems.at[3]))
    for copy in copies:
        copy.start()
    for part in range(3):
        copies[part].wait()
        for r, row in enumerate(natural_to_rows(scratch.at[part], natural.at[part])):
            own[part, r] = row
    copies[3].wait()
    mark = shift_row(flow, 0, pairs, lanes)
    first_one[3 * RIM] = mark
    first_two[3 * RIM] = mark
    for last, first, chosen in (
        (first_one, first_two, place.even),
        (first_two, first_one, jnp.logical_not(place.even)),
    ):

        @pl.when(chosen)
        def _():
            for part in range(3):
                last[part * RIM : (part + 1) * RIM] = own[part, rows - RIM : rows]
                first[part * RIM : (part + 1) * RIM] = own[part, 0:RIM]


def frame_kernel(flow_in, features, *rest):
    *framed, natural, scratch, sems, flow = rest
    _, pairs, lanes = framed[0].shape
    rows = framed[0].shape[0] - 2
    copies = [
        pltpu.make_async_copy(features.at[later + 1], natural.at[later], sems.at[later])
        for later in range(len(framed))
    ]
    copies.append(pltpu.make_async_copy(flow_in, flow, sems.at[len(framed)]))
    for copy in copies:
        copy.start()
    for later, frame in enumerate(framed):
        copies[later].wait()
        for r, row in enumerate(natural_to_rows(scratch.at[later], natural.at[later])):
            frame[1 + r] = row
    copies[-1].wait()
    for later, frame in enumerate(framed):
        mark = shift_row(flow, later + 1, pairs, lanes)
        frame[0] = mark
        frame[rows + 1] = mark


def start_kernel(slots, index, clip, flow, own, w_ref, acc, ops, padded):
    _, rows, _, lanes = own.shape
    place = Place(index, clip, slots)
    low, sub = lane_low(lanes), sublane(lanes)
    clear_pads(padded)
    keep = place.keep(0)
    for part in range(2):
        for r in range(rows):
            stage(padded, part * rows + r, jnp.where(keep, own[part, r].astype(F32), 0.0), False)
            put_warped(ops, (part, r), padded, part * rows + r, flow[0, part, 0], low, sub)
    for r in range(rows):
        stage(padded, 2 * rows + r, own[2, r].astype(F32), False)
        put_plain(ops, (2, r), padded, 2 * rows + r, low)
    first, end = local_span(rows)
    fetches = [lambda r, h, part=part: ops[part, r - RIM, h] for part in range(3)]
    acc[...] = two_row_conv(fetches, first, end - first, w_ref, (0, 1, 2))


def rows_to_natural(natural, plain_rows):
    rows, pairs, lanes = plain_rows.shape
    groups = pairs // SUB
    flat = plain_rows.reshape(rows * pairs, lanes)
    for v in range(groups):
        for s in range(SUB):
            pair = groups * s + v
            tile = flat[pl.ds(SUB * v + s, rows, stride=pairs), :]
            natural[:, pair * lanes : (pair + 1) * lanes] = tile.astype(BF16)


def ahead_kernel(
    slots, tick, interleaved, index, clip, latest, prev, prev_one, prev_two,
    feat, feat_above, feat_below, w_ref, acc, ops, shifts, natural,
    padded, padded_latest, window, plain_rows, *copying,
):
    rows, pairs, lanes = latest.shape
    place = Place(index, clip, slots)
    even = place.even
    low, sub = lane_low(lanes), sublane(lanes)
    keep_latest = place.keep(tick)
    keep_earlier = keep_latest & place.keep(tick - 1)
    own_shift = scalars_of(feat[0])
    above_shift = scalars_of(feat_above[RIM])
    below_shift = scalars_of(feat_below[0])
    shifts[0] = above_shift[0]
    shifts[1] = below_shift[0]
    clear_pads(padded)
    clear_pads(padded_latest)
    span = rows + 2 * RIM
    for r in range(span):
        if r < RIM:
            row, ok = feat_above[r].astype(F32), place.above
        elif r < RIM + rows:
            row, ok = feat[1 + r - RIM].astype(F32), None
        else:
            row, ok = feat_below[1 + r - RIM - rows].astype(F32), place.below
        stage(padded, r, row if ok is None else jnp.where(ok, row, 0.0), False)
        put_plain(window, (1, r), padded, r, low)
    for r in range(span):
        at = span + r
        if r < RIM:
            row = jnp.where(even, prev_two[r], prev_one[r])
            ok, shift = place.above & keep_earlier, above_shift[1]
        elif r < RIM + rows:
            row = prev[r - RIM]
            ok, shift = keep_earlier, own_shift[1]
        else:
            q = r - RIM - rows
            row = jnp.where(even, prev_one[q], prev_two[q])
            ok, shift = place.below & keep_earlier, below_shift[1]
        stage(padded, at, jnp.where(ok, row.astype(F32), 0.0), interleaved)
        put_warped(window, (0, r), padded, at, shift, low, sub)
    for r in range(rows):
        row = latest[r].astype(F32)
        plain_rows[r] = row
        stage(padded_latest, r, jnp.where(keep_latest, row, 0.0), True)
        put_warped(ops, (0, r), padded_latest, r, own_shift[0], low, sub)
    count = (span - 2) // 2
    first, end = local_span(rows)
    known = [lambda r, h: window[0, r, h], lambda r, h: window[1, r, h]]
    latest_own = [lambda r, h: ops[0, r - RIM, h]]
    for begin, stop, fetches, layers in (
        (0, first, known, (1, 2)),
        (first, end, latest_own + known, (0, 1, 2)),
        (end, count, known, (1, 2)),
    ):
        acc[begin * pairs : stop * pairs] = two_row_conv(
            fetches, begin, stop - begin, w_ref, layers
        )
    if copying:
        natural_rows, sem = copying
        rows_to_natural(natural_rows, plain_rows)
        copy = pltpu.make_async_copy(natural_rows, natural.at[0], sem)
        copy.start()
        copy.wait()
    else:
        rows_to_natural(natural, plain_rows)


def finish_kernel(
    slots, tick, index, clip, shifts, acc_in, ops, halo_one, halo_two, w_ref,
    latest, natural, sends, window, layers, padded, plain_rows,
):
    parts, rows, _, pairs, lanes = ops.shape
    place = Place(index, clip, slots)
    even = place.even
    low, sub = lane_low(lanes), sublane(lanes)
    keep = place.keep(tick)
    if tick == 0:
        marks = parts * RIM
        above_shift = scalars_of(jnp.where(even, halo_two[marks], halo_one[marks]))
        below_shift = scalars_of(jnp.where(even, halo_one[marks], halo_two[marks]))
    else:
        above_shift = (shifts[0],)
        below_shift = (shifts[1],)
    clear_pads(padded)
    order = [("above", r) for r in range(RIM)] + [("below", r) for r in range(RIM)]
    at = 0
    for where, r in order:
        for part in range(parts):
            near, far = (halo_two, halo_one) if where == "above" else (halo_one, halo_two)
            ok = place.above if where == "above" else place.below
            shift = above_shift if where == "above" else below_shift
            slot = r if where == "above" else RIM + r
            row = jnp.where(even, near[part * RIM + r], far[part * RIM + r]).astype(F32)
            if part < 2:
                ok = ok & keep
            stage(padded, at, jnp.where(ok, row, 0.0), tick > 0)
            if part < 2:
                put_warped(window, (part, slot), padded, at, shift[part], low, sub)
            else:
                put_plain(window, (part, slot), padded, at, low)
            at += 1

    def operand(part):
        def fetch(r, h):
            if r < RIM:
                return window[part, r, h]
            if r < RIM + rows:
                return ops[part, r - RIM, h]
            return window[part, r - rows, h]

        return fetch

    count = (rows + 2 * RIM - 2) // 2
    first, end = local_span(rows)
    split = end

    def emit(layer, pair, both):
        margin = RIM - 1 - layer
        for q in range(2):
            r = 2 * pair + q
            value = both[:, q * lanes : (q + 1) * lanes]
            if layer == 0:
                value = jnp.maximum(value, 0.1 * value)
            elif layer % 2 == 1:
                value = jnp.maximum(value, 0.0)
            else:
                value = value + layers[layer - 2][r + 2, 0].astype(F32)
            if r < margin:
                value = jnp.where(place.above, value, 0.0)
            elif r >= margin + rows:
                value = jnp.where(place.below, value, 0.0)
            if layer < 2 * RES_BLOCKS:
                put(layers[layer], (r,), value, low, sub)
            else:
                if sends:
                    latest[r] = value.astype(BF16)
                else:
                    plain_rows[r] = value

    fetches = [operand(part) for part in range(parts)]
    join = tuple(range(parts))
    for begin, stop in ((0, first), (first, end), (end, count)):
        made = None
        if begin != first:
            made = two_row_conv(fetches, begin, stop - begin, w_ref, join)
        for k in range(begin, stop):
            if begin == first:
                at = k - first if tick == 0 else k
                both = acc_in[at * pairs : (at + 1) * pairs]
            else:
                both = made[(k - begin) * pairs : (k - begin + 1) * pairs]
                if tick > 0:
                    both = both + acc_in[k * pairs : (k + 1) * pairs]
            emit(0, k, both)
    for layer in range(1, 2 * RES_BLOCKS + 1):
        count -= 1
        split -= 1
        for begin, stop in ((0, split), (split, count)):
            made = two_row_conv(
                [lambda r, h: layers[layer - 1][r, h]], begin, stop - begin, w_ref, (2 + layer,)
            )
            for k in range(begin, stop):
                emit(layer, k, made[(k - begin) * pairs : (k - begin + 1) * pairs])
    if not sends:
        rows_to_natural(natural, plain_rows)
        return
    send_one, send_two = sends

    @pl.when(even)
    def _():
        send_one[...] = latest[rows - RIM : rows]
        send_two[...] = latest[0:RIM]

    @pl.when(jnp.logical_not(even))
    def _():
        send_one[...] = latest[0:RIM]
        send_two[...] = latest[rows - RIM : rows]


def pair_weights(weight):
    before, here, after = weight[:, :, 0], weight[:, :, 1], weight[:, :, 2]
    zero = jnp.zeros_like(here)
    return jnp.concatenate(
        [
            jnp.concatenate([here, before], axis=-1),
            jnp.concatenate([after, here], axis=-1),
            jnp.concatenate([zero, after], axis=-1),
            jnp.concatenate([before, zero], axis=-1),
        ],
        axis=2,
    )


def all_weights(join_weight, res_weight, channels):
    return jnp.concatenate(
        [
            pair_weights(
                join_weight.reshape(3, 3, 3, channels, channels).transpose(2, 0, 1, 3, 4)
            ),
            pair_weights(res_weight.reshape(2 * RES_BLOCKS, 3, 3, channels, channels)),
        ],
        axis=0,
    )


def shards(features, carried, flow_shift, clip_start, join_weight, res_weight):
    rows = features.shape[1]
    wide = features.shape[2]
    channels = join_weight.shape[2]
    lanes = 2 * channels
    pairs = wide // lanes
    slots = lax.axis_size("rows")
    bands = slots // SECTIONS
    lead = bands // 2
    index = lax.axis_index("rows")
    even = (index + (slots - lead)) % 2 == 0
    index = index.astype(jnp.int32).reshape(1)

    def route(move):
        return [(i, move(i) % slots) for i in range(slots)]

    def is_even(i):
        return (i - lead) % 2 == 0

    swap_one = route(lambda i: i + 1 if is_even(i) else i - 1)
    swap_two = route(lambda i: i - 1 if is_even(i) else i + 1)

    def shift_by(count):
        return route(lambda i: i + count)

    def send(block, path):
        return lax.ppermute(block, "rows", path)

    flow = jnp.transpose(flow_shift, (1, 2, 0))
    made = rows + 2 * (RIM - 1)
    total = made // 2 * pairs
    span = rows + 2 * RIM
    long = pairs + 2 * PAD
    first, end = local_span(rows)
    params = pltpu.CompilerParams(vmem_limit_bytes=GRANT)

    def cost(pairs_done, depth):
        return pl.CostEstimate(
            flops=pairs_done * pairs * depth * 16 * lanes * lanes,
            bytes_accessed=4 << 20,
            transcendentals=0,
        )

    def operands(*lead_shape):
        return lead_shape + (2, pairs, lanes)

    def pack():
        def kernel(*refs):
            pack_kernel(slots, *refs)

        halo = jax.ShapeDtypeStruct((3 * RIM + 1, pairs, lanes), BF16)
        return pl.pallas_call(
            kernel,
            out_shape=(jax.ShapeDtypeStruct((3, rows, pairs, lanes), BF16), halo, halo),
            in_specs=[SMEM, HBM, HBM, HBM],
            out_specs=(VMEM, VMEM, VMEM),
            scratch_shapes=[
                pltpu.VMEM((3, rows, wide), BF16),
                pltpu.VMEM((3, rows * (pairs + SUB), lanes), F32),
                pltpu.SemaphoreType.DMA((4,)),
                pltpu.SMEM(flow.shape, jnp.int32),
            ],
            compiler_params=params,
            name="pack",
        )(index, in_hbm(flow), in_hbm(carried), in_hbm(features))

    def frames(features):
        later = TICKS - 1
        frame = jax.ShapeDtypeStruct((rows + 2, pairs, lanes), BF16)
        return pl.pallas_call(
            frame_kernel,
            out_shape=(frame,) * later,
            in_specs=[HBM, HBM],
            out_specs=(VMEM,) * later,
            scratch_shapes=[
                pltpu.VMEM((later, rows, wide), BF16),
                pltpu.VMEM((later, rows * (pairs + SUB), lanes), F32),
                pltpu.SemaphoreType.DMA((later + 1,)),
                pltpu.SMEM(flow.shape, jnp.int32),
            ],
            compiler_params=params,
            name="frame",
        )(in_hbm(flow), in_hbm(features))

    def start(own):
        def kernel(*refs):
            start_kernel(slots, *refs)

        return pl.pallas_call(
            kernel,
            out_shape=(
                jax.ShapeDtypeStruct(((end - first) * pairs, 2 * lanes), F32),
                jax.ShapeDtypeStruct(operands(3, rows), BF16),
            ),
            in_specs=[SMEM, SMEM, SMEM, VMEM, VMEM],
            out_specs=(VMEM, VMEM),
            scratch_shapes=[pltpu.VMEM((3 * rows, long, lanes), F32)],
            compiler_params=params,
            cost_estimate=cost(end - first, 3),
            name="start",
        )(index, clip_start, flow, own, weights)

    def ahead(tick, latest, prev, prev_one, prev_two, feats):
        def kernel(*refs):
            ahead_kernel(slots, tick, tick > 1, *refs)

        whole = (TICKS,) if tick == 1 else ()
        return pl.pallas_call(
            kernel,
            out_shape=(
                jax.ShapeDtypeStruct((total, 2 * lanes), F32),
                jax.ShapeDtypeStruct(operands(1, rows), BF16),
                jax.ShapeDtypeStruct((2,), jnp.int32),
                jax.ShapeDtypeStruct(whole + (rows, wide), BF16),
            ),
            in_specs=[SMEM, SMEM] + [VMEM] * 8,
            out_specs=(VMEM, VMEM, SMEM, HBM if whole else VMEM),
            scratch_shapes=[
                pltpu.VMEM((2 * span, long, lanes), F32),
                pltpu.VMEM((rows, long, lanes), F32),
                pltpu.VMEM(operands(2, span), BF16),
                pltpu.VMEM((rows, pairs, lanes), F32),
            ]
            + ([pltpu.VMEM((rows, wide), BF16), pltpu.SemaphoreType.DMA] if whole else []),
            compiler_params=params,
            cost_estimate=cost(made, 1),
        )(index, clip_start, latest, prev, prev_one, prev_two, *feats, weights)

    def finish(tick, shifts, acc, ops, one, two):
        last = tick + 1 == TICKS
        parts = ops.shape[0]

        def kernel(index, clip, shifts, acc_in, ops, one, two, w_ref, *rest):
            if last:
                natural, *scratch = rest
                latest, sends = None, ()
            else:
                latest, send_one, send_two, *scratch = rest
                natural, sends = None, (send_one, send_two)
            window, *layers, padded, plain_rows = scratch
            finish_kernel(
                slots, tick, index, clip, shifts, acc_in, ops, one, two, w_ref,
                latest, natural, sends, window, layers, padded, plain_rows,
            )

        halo = jax.ShapeDtypeStruct((RIM, pairs, lanes), BF16)
        if last:
            outs = (jax.ShapeDtypeStruct((rows, wide), BF16),)
        else:
            outs = (jax.ShapeDtypeStruct((rows, pairs, lanes), BF16), halo, halo)
        return pl.pallas_call(
            kernel,
            out_shape=outs,
            in_specs=[SMEM, SMEM, SMEM] + [VMEM] * 5,
            out_specs=(VMEM,) * len(outs),
            scratch_shapes=[pltpu.VMEM(operands(parts, 2 * RIM), BF16)]
            + [pltpu.VMEM(operands(made - 2 * layer), BF16) for layer in range(2 * RES_BLOCKS)]
            + [
                pltpu.VMEM((parts * 2 * RIM, long, lanes), F32),
                pltpu.VMEM((rows, pairs, lanes), F32),
            ],
            compiler_params=params,
            cost_estimate=cost(made + made // 2 * parts, 1),
        )(index, clip_start, shifts, acc, ops, one, two, weights)

    own, first_one, first_two = pack()
    later_features, first_one, first_two = lax.optimization_barrier(
        (features, first_one, first_two)
    )
    halo_two = send(first_two, swap_two)
    halo_one = send(first_one, swap_one)
    framed = frames(later_features)
    framed, own, join_weight, res_weight = lax.optimization_barrier(
        (framed, own, join_weight, res_weight)
    )
    feats = [[] for _ in range(TICKS)]
    for tick in range(1, TICKS):
        frame = framed[tick - 1]
        back = -bands * tick
        feats[tick].append(send(frame, shift_by(back)))
        if tick == 1:
            feats[tick].append(send(frame[rows + 1 - RIM :], shift_by(back + 1)))
            feats[tick].append(send(frame[: RIM + 1], shift_by(back - 1)))
    weights = all_weights(join_weight, res_weight, channels)
    acc, ops = start(own)
    latest, send_one, send_two = finish(
        0, jnp.zeros((2,), jnp.int32), acc, ops, halo_one, halo_two
    )
    prev, prev_one, prev_two = own[0], halo_one, halo_two
    for tick in range(1, TICKS):
        two = send(send_two, swap_two)
        one = send(send_one, swap_one)
        acc, ops, shifts, natural = ahead(tick, latest, prev, prev_one, prev_two, feats[tick])
        if tick == 1:
            result = natural
        else:
            moved = send(natural, shift_by(bands * (tick - 1)))
            result = lax.dynamic_update_slice_in_dim(result, moved[None], tick - 1, 0)
        if tick + 1 < TICKS:
            acc, frame = lax.optimization_barrier((acc, feats[tick + 1][0]))
            begin_one = jnp.where(even, rows + 1 - RIM, 0)
            begin_two = jnp.where(even, 0, rows + 1 - RIM)
            size = RIM + 1
            part_two = lax.dynamic_slice_in_dim(frame, begin_two, size, axis=0)
            part_one = lax.dynamic_slice_in_dim(frame, begin_one, size, axis=0)
            frame_two = send(part_two, swap_two)
            frame_one = send(part_one, swap_one)
            feats[tick + 1] = [
                frame,
                jnp.where(even, frame_two, frame_one),
                jnp.where(even, frame_one, frame_two),
            ]
        prev, prev_one, prev_two = latest, one, two
        outs = finish(tick, shifts, acc, ops, one, two)
        if tick + 1 < TICKS:
            latest, send_one, send_two = outs
    moved = send(outs[0], shift_by(bands * (TICKS - 1)))
    return lax.dynamic_update_slice_in_dim(result, moved[None], TICKS - 1, 0)


def solution(mesh):
    in_specs = (
        P(None, ("groups", "rows"), None),
        P(None, ("groups", "rows"), None),
        P(None, ("groups", "rows"), None),
        P("groups"),
        P(),
        P(),
    )
    out_specs = P(None, ("groups", "rows"), None)

    return jax.shard_map(shards, mesh=mesh, in_specs=in_specs, out_specs=out_specs, check_vma=False)
```

profile of v0, /device:TPU:0, one launch (start us, length us, event | category | flops | bytes accessed | tf_op | source)
XLA Modules:
  0.0 59.8 jit_solution(8083938740993890956)
XLA Ops:
  0.0 1.9 %pack.1 = (bf16[3,8,64,128]{3,2,1,0:T(8,128)(2,1)S(1)}, bf16[16,64,128]{2,1,0:T(8,128)(2,1)}, bf16[16,64,128]{2,1,0:T(8,128)(2,1)S(1)}) custom-call(s32[1]{0:T(128)} %bitcast.refs_0_.index, s32[1,2,3]{2,1,0:T(2,128)} %bitcast.31, bf16[2,8,8192]{2,1,0:T(8,128)(2,1)} %refs_2_.1, bf16[3,8,8192]{2,1,0:T(8,128)(2,1)} %features), custom_call_target="tpu_custom_call" | custom-call | tf_op jit(solution)/shard_map/pack/pallas_call | solution.py:510
  1.9 0.6 collective-permute-start
  2.5 5.7 %collective-permute-start.1 = (bf16[16,64,128]{2,1,0:T(8,128)(2,1)S(1)}, bf16[16,64,128]{2,1,0:T(8,128)(2,1)S(1)}, u32[]{:S(2)}, u32[]{:S(2)}) collective-permute-start(bf16[16,64,128]{2,1,0:T(8,128)(2,1)S(1)} %get-tuple-element.48), channel_id=1, source_target_pairs={{0,15},{1,2},{2,1},{3,4},{4,3},{5,6},{6,5},{7,8},{8,7},{9,10},{10,... | collective-permute-start | bytes 786440 | tf_op jit(solution)/shard_map/ppermute | solution.py:485
  8.1 1.1 %frame.1 = (bf16[10,64,128]{2,1,0:T(8,128)(2,1)S(1)}, bf16[10,64,128]{2,1,0:T(8,128)(2,1)S(1)}) custom-call(s32[1,2,3]{2,1,0:T(2,128)} %bitcast.32, bf16[3,8,8192]{2,1,0:T(8,128)(2,1)} %features), custom_call_target="tpu_custom_call" | custom-call | tf_op jit(solution)/shard_map/frame/pallas_call | solution.py:528
  9.2 0.0 copy-start.2
  9.2 0.5 collective-permute-start.2
  9.7 0.7 %fusion.19 = (bf16[6,64,128]{2,1,0:T(8,128)(2,1)}, bf16[6,64,128]{2,1,0:T(8,128)(2,1)}) fusion(bf16[10,64,128]{2,1,0:T(8,128)(2,1)S(1)} %get-tuple-element.50), kind=kLoop, calls=%fused_computation.38 | loop fusion | bytes 393216 | tf_op jit(solution)/shard_map/slice | solution.py:641
  10.4 0.0 collective-permute-start.3
  10.4 0.6 %collective-permute-start.4 = (bf16[6,64,128]{2,1,0:T(8,128)(2,1)}, bf16[6,64,128]{2,1,0:T(8,128)(2,1)S(1)}, u32[]{:S(2)}, u32[]{:S(2)}) collective-permute-start(bf16[6,64,128]{2,1,0:T(8,128)(2,1)} %get-tuple-element.77), channel_id=1, source_target_pairs={{0,11},{1,12},{2,13},{3,14},{4,15},{5,0},{6,1},{7,2},{8,3},{9,4},{... | collective-permute-start | bytes 294920 | tf_op jit(solution)/shard_map/ppermute | solution.py:485
  11.0 0.0 copy-done.3
  11.1 0.2 copy.7
  11.3 0.8 %slice_bitcast_fusion.5 = (bf16[3,3,64,64]{3,2,1,0:T(8,128)(2,1)S(1)}, bf16[3,3,64,64]{3,2,1,0:T(8,128)(2,1)}, bf16[3,3,64,64]{3,2,1,0:T(8,128)(2,1)}) fusion(bf16[3,3,3,64,64]{4,3,1,0,2:T(8,128)(2,1)S(1)} %bitcast.35), kind=kLoop, calls=%fused_computation.30 | loop fusion | bytes 442368 | tf_op jit(solution)/shard_map/squeeze | solution.py:434
  12.1 0.0 copy-done.2
  12.1 0.3 copy.9
  12.4 0.0 copy-start
  12.5 0.0 copy-start.1
  12.5 2.3 %fusion.16.refs_4_.w_ref.refs_9_ = bf16[7,3,256,128]{3,2,1,0:T(8,128)(2,1)S(1)} fusion(bf16[4,3,64,64]{3,2,1,0:T(8,128)(2,1)S(1)} %get-tuple-element.68, bf16[4,3,64,64]{3,2,1,0:T(8,128)(2,1)S(1)} %get-tuple-element.69, bf16[3,3,64,64]{3,2,1,0:T(8,128)(2,1)} %get-tuple-element.72, bf16[3,3,64,64]{3,2,1,0:T(8,128)(2,1)} %get-tuple-element.71, ...), kind=kLoop, calls=%fused_computation.21 | loop fusion | flops 29589504 | bytes 1892352 | tf_op jit(solution)/shard_map/concatenate | solution.py:448
  14.8 0.0 collective-permute-done.one.refs_4_
  14.8 3.6 %collective-permute-start.5 = (bf16[10,64,128]{2,1,0:T(8,128)(2,1)S(1)}, bf16[10,64,128]{2,1,0:T(8,128)(2,1)S(1)}, u32[]{:S(2)}, u32[]{:S(2)}) collective-permute-start(bf16[10,64,128]{2,1,0:T(8,128)(2,1)S(1)} %get-tuple-element.54), channel_id=1, source_target_pairs={{0,8},{1,9},{2,10},{3,11},{4,12},{5,13},{6,14},{7,15},{8,0},{9,1},... | collective-permute-start | bytes 491528 | tf_op jit(solution)/shard_map/ppermute | solution.py:485
  18.4 1.3 %start.1 = (f32[128,256]{1,0:T(8,128)S(1)}, bf16[3,8,2,64,128]{4,3,2,1,0:T(8,128)(2,1)S(1)}) custom-call(s32[1]{0:T(128)} %bitcast.refs_0_.index, s32[4]{0:T(128)S(1)} %copy-done, s32[1,2,3]{2,1,0:T(2,128)S(1)} %bitcast.33, bf16[3,8,64,128]{3,2,1,0:T(8,128)(2,1)S(1)} %get-tuple-element.42.refs_3_, bf16[7,3,256,128]{3,2,1,0:T(8,128)(2,1)S(1)} %fusion.16.refs_4_.w_ref.refs_9_), custom_call_target="tpu_custom_call" | custom-call | flops 100663296 | bytes 4194304 | tf_op jit(solution)/shard_map/start/pallas_call | solution.py:547
  19.7 0.0 collective-permute-done.1.two.refs_5_
  19.7 3.2 %shard_map.64 = (bf16[8,64,128]{2,1,0:T(8,128)(2,1)S(1)}, bf16[5,64,128]{2,1,0:T(8,128)(2,1)S(1)}, bf16[5,64,128]{2,1,0:T(8,128)(2,1)S(1)}) custom-call(s32[1]{0:T(128)} %bitcast.refs_0_.index, s32[4]{0:T(128)S(1)} %copy-done, s32[2]{0:T(128)S(1)} %broadcast_1_shifts.2.shifts, f32[128,256]{1,0:T(8,128)S(1)} %get-tuple-element.45.acc_in, ...), custom_call_target="tpu_custom_call" | custom-call | flops 671088640 | bytes 4194304 | tf_op jit(solution)/shard_map/pallas_call | solution.py:609
  22.9 0.0 collective-permute-done.3.refs_7_
  22.9 0.0 collective-permute-done.4.refs_8_
  22.9 0.0 collective-permute-done.2.refs_6_
  22.9 3.3 %shard_map.65 = (f32[512,256]{1,0:T(8,128)S(1)}, bf16[1,8,2,64,128]{4,3,2,1,0:T(8,128)(2,1)S(1)}, s32[2]{0:T(128)S(1)}, bf16[3,8,8192]{2,1,0:T(8,128)(2,1)}) custom-call(s32[1]{0:T(128)} %bitcast.refs_0_.index, s32[4]{0:T(128)S(1)} %copy-done, bf16[8,64,128]{2,1,0:T(8,128)(2,1)S(1)} %get-tuple-element.49.refs_2_.refs_3_, ...), custom_call_target="tpu_custom_call" | custom-call | flops 268435456 | bytes 4194304 | tf_op jit(solution)/shard_map/pallas_call | solution.py:566
  26.2 1.5 %collective-permute-done.5.refs_6_ = bf16[10,64,128]{2,1,0:T(8,128)(2,1)S(1)} collective-permute-done((bf16[10,64,128]{2,1,0:T(8,128)(2,1)S(1)}, bf16[10,64,128]{2,1,0:T(8,128)(2,1)S(1)}, u32[]{:S(2)}, u32[]{:S(2)}) %collective-permute-start.5) | collective-permute-done | bytes 163872 | tf_op jit(solution)/shard_map/ppermute | solution.py:485
  27.7 0.0 collective-permute-start.6
  27.7 5.6 %collective-permute-start.7 = (bf16[5,64,128]{2,1,0:T(8,128)(2,1)S(1)}, bf16[5,64,128]{2,1,0:T(8,128)(2,1)S(1)}, u32[]{:S(2)}, u32[]{:S(2)}) collective-permute-start(bf16[5,64,128]{2,1,0:T(8,128)(2,1)S(1)} %get-tuple-element.58), channel_id=1, source_target_pairs={{0,15},{1,2},{2,1},{3,4},{4,3},{5,6},{6,5},{7,8},{8,7},{9,10},{10,... | collective-permute-start | bytes 245768 | tf_op jit(solution)/shard_map/ppermute | solution.py:485
  33.4 0.1 collective-permute-start.8
  33.5 0.1 collective-permute-start.9
  33.5 0.0 collective-permute-done.6.one.refs_4_
  33.5 2.0 %collective-permute-done.7.two.refs_5_ = bf16[5,64,128]{2,1,0:T(8,128)(2,1)S(1)} collective-permute-done((bf16[5,64,128]{2,1,0:T(8,128)(2,1)S(1)}, bf16[5,64,128]{2,1,0:T(8,128)(2,1)S(1)}, u32[]{:S(2)}, u32[]{:S(2)}) %collective-permute-start.7) | collective-permute-done | bytes 81952 | tf_op jit(solution)/shard_map/ppermute | solution.py:485
  35.5 2.4 %shard_map.66 = (bf16[8,64,128]{2,1,0:T(8,128)(2,1)S(1)}, bf16[5,64,128]{2,1,0:T(8,128)(2,1)S(1)}, bf16[5,64,128]{2,1,0:T(8,128)(2,1)S(1)}) custom-call(s32[1]{0:T(128)} %bitcast.refs_0_.index, s32[4]{0:T(128)S(1)} %copy-done, s32[2]{0:T(128)S(1)} %get-tuple-element.52.shifts, f32[512,256]{1,0:T(8,128)S(1)} %get-tuple-element.55.acc_in, ...), custom_call_target="tpu_custom_call" | custom-call | flops 402653184 | bytes 4194304 | tf_op jit(solution)/shard_map/pallas_call | solution.py:609
  37.9 2.3 %collective-permute-done.8 = bf16[6,64,128]{2,1,0:T(8,128)(2,1)S(1)} collective-permute-done((bf16[6,64,128]{2,1,0:T(8,128)(2,1)S(1)}, bf16[6,64,128]{2,1,0:T(8,128)(2,1)S(1)}, u32[]{:S(2)}, u32[]{:S(2)}) %collective-permute-start.8) | collective-permute-done | bytes 98336 | tf_op jit(solution)/shard_map/ppermute | solution.py:485
  40.2 0.0 collective-permute-done.9
  40.2 2.1 %shard_map.67 = (f32[512,256]{1,0:T(8,128)S(1)}, bf16[1,8,2,64,128]{4,3,2,1,0:T(8,128)(2,1)S(1)}, s32[2]{0:T(128)S(1)}, bf16[8,8192]{1,0:T(8,128)(2,1)S(1)}) custom-call(s32[1]{0:T(128)} %bitcast.refs_0_.index, s32[4]{0:T(128)S(1)} %copy-done, bf16[8,64,128]{2,1,0:T(8,128)(2,1)S(1)} %get-tuple-element.59.refs_2_, ...), custom_call_target="tpu_custom_call" | custom-call | flops 268435456 | bytes 4194304 | tf_op jit(solution)/shard_map/pallas_call | solution.py:566
  42.3 0.1 collective-permute-start.10
  42.4 0.1 collective-permute-start.11
  42.5 2.3 %collective-permute-start.12 = (bf16[5,64,128]{2,1,0:T(8,128)(2,1)S(1)}, bf16[5,64,128]{2,1,0:T(8,128)(2,1)S(1)}, u32[]{:S(2)}, u32[]{:S(2)}) collective-permute-start(bf16[5,64,128]{2,1,0:T(8,128)(2,1)S(1)} %get-tuple-element.66), channel_id=1, source_target_pairs={{0,15},{1,2},{2,1},{3,4},{4,3},{5,6},{6,5},{7,8},{8,7},{9,10},{10,... | collective-permute-start | bytes 245768 | tf_op jit(solution)/shard_map/ppermute | solution.py:485
  44.7 0.0 collective-permute-done.11.one
  44.7 4.4 %collective-permute-done.12.two = bf16[5,64,128]{2,1,0:T(8,128)(2,1)S(1)} collective-permute-done((bf16[5,64,128]{2,1,0:T(8,128)(2,1)S(1)}, bf16[5,64,128]{2,1,0:T(8,128)(2,1)S(1)}, u32[]{:S(2)}, u32[]{:S(2)}) %collective-permute-start.12) | collective-permute-done | bytes 81952 | tf_op jit(solution)/shard_map/ppermute | solution.py:485
  49.1 2.5 %shard_map.68 = bf16[8,8192]{1,0:T(8,128)(2,1)S(1)} custom-call(s32[1]{0:T(128)} %bitcast.refs_0_.index, s32[4]{0:T(128)S(1)} %copy-done, s32[2]{0:T(128)S(1)} %get-tuple-element.62.shifts, f32[512,256]{1,0:T(8,128)S(1)} %get-tuple-element.63.acc_in, bf16[1,8,2,64,128]{4,3,2,1,0:T(8,128)(2,1)S(1)} %get-tuple-element.64.ops, ...), custom_call_target="tpu_custom_call" | custom-call | flops 402653184 | bytes 4194304 | tf_op jit(solution)/shard_map/pallas_call | solution.py:609
  51.6 0.1 collective-permute-start.13
  51.7 0.0 collective-permute-done.10
  51.7 0.7 %bitcast_dynamic-update-slice_fusion.1 = bf16[3,8,8192]{2,1,0:T(8,128)(2,1)} fusion(bf16[3,8,8192]{2,1,0:T(8,128)(2,1)} %get-tuple-element.51, bf16[8,8192]{1,0:T(8,128)(2,1)S(1)} %collective-permute-done.10), kind=kLoop, calls=%fused_computation.32 | loop fusion | bytes 262144 | tf_op jit(solution)/shard_map/dynamic_update_slice | solution.py:656
  52.4 6.7 %collective-permute-done.13 = bf16[8,8192]{1,0:T(8,128)(2,1)S(1)} collective-permute-done((bf16[8,8192]{1,0:T(8,128)(2,1)S(1)}, bf16[8,8192]{1,0:T(8,128)(2,1)S(1)}, u32[]{:S(2)}, u32[]{:S(2)}) %collective-permute-start.13) | collective-permute-done | bytes 131104 | tf_op jit(solution)/shard_map/ppermute | solution.py:485
  59.1 0.7 %bitcast_dynamic-update-slice_fusion = bf16[3,8,8192]{2,1,0:T(8,128)(2,1)} fusion(bf16[3,8,8192]{2,1,0:T(8,128)(2,1)} %bitcast_dynamic-update-slice_fusion.1, bf16[8,8192]{1,0:T(8,128)(2,1)S(1)} %collective-permute-done.13), kind=kLoop, calls=%fused_computation.31 | loop fusion | bytes 262144 | tf_op jit(solution)/shard_map/dynamic_update_slice | solution.py:676
  (9 shorter events, 0.1 us)
Async XLA Ops:
  0.0 11.0 %copy-start.3 = (bf16[3,576,64]{1,2,0:T(8,128)(2,1)S(1)}, bf16[3,576,64]{1,2,0:T(8,128)(2,1)}, u32[]{:S(2)}) copy-start(bf16[3,576,64]{1,2,0:T(8,128)(2,1)} %param.10) | copy-start | bytes 663556
  1.9 12.8 %collective-permute-start = (bf16[16,64,128]{2,1,0:T(8,128)(2,1)}, bf16[16,64,128]{2,1,0:T(8,128)(2,1)S(1)}, u32[]{:S(2)}, u32[]{:S(2)}) collective-permute-start(bf16[16,64,128]{2,1,0:T(8,128)(2,1)} %get-tuple-element.47), channel_id=1, source_target_pairs={{0,1},{1,0},{2,3},{3,2},{4,5},{5,4},{6,7},{7,6},{8,9},{9,8},{10,11... | collective-permute-start | bytes 786440 | tf_op jit(solution)/shard_map/ppermute | solution.py:485
  2.5 17.2 %collective-permute-start.1 = (bf16[16,64,128]{2,1,0:T(8,128)(2,1)S(1)}, bf16[16,64,128]{2,1,0:T(8,128)(2,1)S(1)}, u32[]{:S(2)}, u32[]{:S(2)}) collective-permute-start(bf16[16,64,128]{2,1,0:T(8,128)(2,1)S(1)} %get-tuple-element.48), channel_id=1, source_target_pairs={{0,15},{1,2},{2,1},{3,4},{4,3},{5,6},{6,5},{7,8},{8,7},{9,10},{10,... | collective-permute-start | bytes 786440 | tf_op jit(solution)/shard_map/ppermute | solution.py:485
  9.2 2.9 %copy-start.2 = (bf16[4,3,192,64]{2,3,1,0:T(8,128)(2,1)S(1)}, bf16[4,3,192,64]{2,3,1,0:T(8,128)(2,1)}, u32[]{:S(2)}) copy-start(bf16[4,3,192,64]{2,3,1,0:T(8,128)(2,1)} %param.11) | copy-start | bytes 884740
  9.2 13.7 %collective-permute-start.2 = (bf16[10,64,128]{2,1,0:T(8,128)(2,1)S(1)}, bf16[10,64,128]{2,1,0:T(8,128)(2,1)S(1)}, u32[]{:S(2)}, u32[]{:S(2)}) collective-permute-start(bf16[10,64,128]{2,1,0:T(8,128)(2,1)S(1)} %get-tuple-element.50), channel_id=1, source_target_pairs={{0,12},{1,13},{2,14},{3,15},{4,0},{5,1},{6,2},{7,3},{8,4},{9,5},{1... | collective-permute-start | bytes 491528 | tf_op jit(solution)/shard_map/ppermute | solution.py:485
  10.4 12.4 %collective-permute-start.3 = (bf16[6,64,128]{2,1,0:T(8,128)(2,1)}, bf16[6,64,128]{2,1,0:T(8,128)(2,1)S(1)}, u32[]{:S(2)}, u32[]{:S(2)}) collective-permute-start(bf16[6,64,128]{2,1,0:T(8,128)(2,1)} %get-tuple-element.78), channel_id=1, source_target_pairs={{0,13},{1,14},{2,15},{3,0},{4,1},{5,2},{6,3},{7,4},{8,5},{9,6},{10... | collective-permute-start | bytes 294920 | tf_op jit(solution)/shard_map/ppermute | solution.py:485
  10.4 12.4 %collective-permute-start.4 = (bf16[6,64,128]{2,1,0:T(8,128)(2,1)}, bf16[6,64,128]{2,1,0:T(8,128)(2,1)S(1)}, u32[]{:S(2)}, u32[]{:S(2)}) collective-permute-start(bf16[6,64,128]{2,1,0:T(8,128)(2,1)} %get-tuple-element.77), channel_id=1, source_target_pairs={{0,11},{1,12},{2,13},{3,14},{4,15},{5,0},{6,1},{7,2},{8,3},{9,4},{... | collective-permute-start | bytes 294920 | tf_op jit(solution)/shard_map/ppermute | solution.py:485
  12.4 5.9 %copy-start = (s32[4]{0:T(128)S(1)}, s32[4]{0:T(128)}, u32[]{:S(2)}) copy-start(s32[4]{0:T(128)} %clip.5) | copy-start | bytes 52
  12.5 5.9 %copy-start.1 = (s32[3,1,2]{0,2,1:T(2,128)S(1)}, s32[3,1,2]{0,2,1:T(2,128)}, u32[]{:S(2)}) copy-start(s32[3,1,2]{0,2,1:T(2,128)} %param.8) | copy-start | bytes 76
  14.8 12.9 %collective-permute-start.5 = (bf16[10,64,128]{2,1,0:T(8,128)(2,1)S(1)}, bf16[10,64,128]{2,1,0:T(8,128)(2,1)S(1)}, u32[]{:S(2)}, u32[]{:S(2)}) collective-permute-start(bf16[10,64,128]{2,1,0:T(8,128)(2,1)S(1)} %get-tuple-element.54), channel_id=1, source_target_pairs={{0,8},{1,9},{2,10},{3,11},{4,12},{5,13},{6,14},{7,15},{8,0},{9,1},... | collective-permute-start | bytes 491528 | tf_op jit(solution)/shard_map/ppermute | solution.py:485
  27.7 5.8 %collective-permute-start.6 = (bf16[5,64,128]{2,1,0:T(8,128)(2,1)S(1)}, bf16[5,64,128]{2,1,0:T(8,128)(2,1)S(1)}, u32[]{:S(2)}, u32[]{:S(2)}) collective-permute-start(bf16[5,64,128]{2,1,0:T(8,128)(2,1)S(1)} %get-tuple-element.57), channel_id=1, source_target_pairs={{0,1},{1,0},{2,3},{3,2},{4,5},{5,4},{6,7},{7,6},{8,9},{9,8},{10,11... | collective-permute-start | bytes 245768 | tf_op jit(solution)/shard_map/ppermute | solution.py:485
  27.7 7.7 %collective-permute-start.7 = (bf16[5,64,128]{2,1,0:T(8,128)(2,1)S(1)}, bf16[5,64,128]{2,1,0:T(8,128)(2,1)S(1)}, u32[]{:S(2)}, u32[]{:S(2)}) collective-permute-start(bf16[5,64,128]{2,1,0:T(8,128)(2,1)S(1)} %get-tuple-element.58), channel_id=1, source_target_pairs={{0,15},{1,2},{2,1},{3,4},{4,3},{5,6},{6,5},{7,8},{8,7},{9,10},{10,... | collective-permute-start | bytes 245768 | tf_op jit(solution)/shard_map/ppermute | solution.py:485
  33.4 6.8 %collective-permute-start.8 = (bf16[6,64,128]{2,1,0:T(8,128)(2,1)S(1)}, bf16[6,64,128]{2,1,0:T(8,128)(2,1)S(1)}, u32[]{:S(2)}, u32[]{:S(2)}) collective-permute-start(bf16[6,64,128]{2,1,0:T(8,128)(2,1)S(1)} %get-tuple-element.76), channel_id=1, source_target_pairs={{0,15},{1,2},{2,1},{3,4},{4,3},{5,6},{6,5},{7,8},{8,7},{9,10},{10,... | collective-permute-start | bytes 294920 | tf_op jit(solution)/shard_map/ppermute | solution.py:485
  33.5 6.7 %collective-permute-start.9 = (bf16[6,64,128]{2,1,0:T(8,128)(2,1)S(1)}, bf16[6,64,128]{2,1,0:T(8,128)(2,1)S(1)}, u32[]{:S(2)}, u32[]{:S(2)}) collective-permute-start(bf16[6,64,128]{2,1,0:T(8,128)(2,1)S(1)} %get-tuple-element.75), channel_id=1, source_target_pairs={{0,1},{1,0},{2,3},{3,2},{4,5},{5,4},{6,7},{7,6},{8,9},{9,8},{10,11... | collective-permute-start | bytes 294920 | tf_op jit(solution)/shard_map/ppermute | solution.py:485
  42.3 9.4 %collective-permute-start.10 = (bf16[8,8192]{1,0:T(8,128)(2,1)S(1)}, bf16[8,8192]{1,0:T(8,128)(2,1)S(1)}, u32[]{:S(2)}, u32[]{:S(2)}) collective-permute-start(bf16[8,8192]{1,0:T(8,128)(2,1)S(1)} %get-tuple-element.61), channel_id=1, source_target_pairs={{0,4},{1,5},{2,6},{3,7},{4,8},{5,9},{6,10},{7,11},{8,12},{9,13},{1... | collective-permute-start | bytes 393224 | tf_op jit(solution)/shard_map/ppermute | solution.py:485
  42.4 2.3 %collective-permute-start.11 = (bf16[5,64,128]{2,1,0:T(8,128)(2,1)S(1)}, bf16[5,64,128]{2,1,0:T(8,128)(2,1)S(1)}, u32[]{:S(2)}, u32[]{:S(2)}) collective-permute-start(bf16[5,64,128]{2,1,0:T(8,128)(2,1)S(1)} %get-tuple-element.65), channel_id=1, source_target_pairs={{0,1},{1,0},{2,3},{3,2},{4,5},{5,4},{6,7},{7,6},{8,9},{9,8},{10,11... | collective-permute-start | bytes 245768 | tf_op jit(solution)/shard_map/ppermute | solution.py:485
  42.5 6.6 %collective-permute-start.12 = (bf16[5,64,128]{2,1,0:T(8,128)(2,1)S(1)}, bf16[5,64,128]{2,1,0:T(8,128)(2,1)S(1)}, u32[]{:S(2)}, u32[]{:S(2)}) collective-permute-start(bf16[5,64,128]{2,1,0:T(8,128)(2,1)S(1)} %get-tuple-element.66), channel_id=1, source_target_pairs={{0,15},{1,2},{2,1},{3,4},{4,3},{5,6},{6,5},{7,8},{8,7},{9,10},{10,... | collective-permute-start | bytes 245768 | tf_op jit(solution)/shard_map/ppermute | solution.py:485
  51.6 7.5 %collective-permute-start.13 = (bf16[8,8192]{1,0:T(8,128)(2,1)S(1)}, bf16[8,8192]{1,0:T(8,128)(2,1)S(1)}, u32[]{:S(2)}, u32[]{:S(2)}) collective-permute-start(bf16[8,8192]{1,0:T(8,128)(2,1)S(1)} %shard_map.68), channel_id=1, source_target_pairs={{0,8},{1,9},{2,10},{3,11},{4,12},{5,13},{6,14},{7,15},{8,0},{9,1},... | collective-permute-start | bytes 393224 | tf_op jit(solution)/shard_map/ppermute | solution.py:485
where the time goes:
time: 60.1 us; the launch traced here: 59.8 us
  starting transfers between devices  19.1 us (32%)
  Pallas kernels  17.8 us (30%)
  waiting for transfers between devices  16.8 us (28%)
  local copies, waits for them, and re-layouts  3.44 us (6%)
  other arithmetic  2.32 us (4%)
    ppermute x14, starting transfers between devices, send(): return lax.ppermute(block, 'rows', path)  19.1 us
    ppermute x14, waiting for transfers between devices, send(): return lax.ppermute(block, 'rows', path)  16.8 us
    pallas_call x3, Pallas kernels, finish(): pl.pallas_call(kernel, out_shape=outs, in_specs=[SMEM, SMEM, SMEM] + [VME...  8.13 us
    pallas_call x2, Pallas kernels, ahead(): pl.pallas_call(kernel, out_shape=(jax.ShapeDtypeStruct((total, 2 * lanes)...  5.41 us
    concatenate x1, other arithmetic, all_weights(): jnp.concatenate([pair_weights(join_weight.reshape(3, 3, 3, channels, chan...  2.3 us
    pallas_call x1, Pallas kernels, pack(): pl.pallas_call(kernel, out_shape=(jax.ShapeDtypeStruct((3, rows, pairs, l...  1.92 us
    pallas_call x1, Pallas kernels, start(): pl.pallas_call(kernel, out_shape=(jax.ShapeDtypeStruct(((end - first) * p...  1.27 us
  transfers between devices with their start and end apart: 14, of which 5 were waited for; matrix products, arithmetic and copies ran while one was open for 8% of the time, Pallas kernels for 23%

commit v1 on v0

--- a/solution.py
+++ b/solution.py
@@ -86,13 +86,15 @@
 
 
 def two_row_weight(w_ref, layers):
-    rows = []
+    zero = jnp.zeros(w_ref.shape[2:], BF16)
+    upper, lower = [], []
     for layer in layers:
-        zero = jnp.zeros(w_ref.shape[2:], BF16)
         w = [w_ref[layer, a] for a in range(3)]
-        for pair in ((w[0], zero), (w[1], w[0]), (w[2], w[1]), (zero, w[2])):
-            rows.append(jnp.concatenate(pair, axis=1))
-    return jnp.concatenate(rows, axis=0)
+        upper += w + [zero]
+        lower += [zero] + w
+    return jnp.concatenate(
+        [jnp.concatenate(upper, axis=1), jnp.concatenate(lower, axis=1)], axis=0
+    )
 
 
 def two_row_conv(fetches, first, count, w_ref, layers):
@@ -105,9 +107,10 @@
                         [fetch(2 * (first + k) + i, part) for k in range(count)], axis=0
                     )
                 )
-    return jnp.dot(
+    return lax.dot_general(
         jnp.concatenate(columns, axis=1),
         two_row_weight(w_ref, layers),
+        (((1,), (1,)), ((), ())),
         preferred_element_type=F32,
     )
 
@@ -220,22 +223,68 @@
         frame[rows + 1] = mark
 
 
-def start_kernel(slots, index, clip, flow, own, w_ref, acc, ops, padded):
-    _, rows, _, lanes = own.shape
-    place = Place(index, clip, slots)
-    low, sub = lane_low(lanes), sublane(lanes)
-    clear_pads(padded)
-    keep = place.keep(0)
-    for part in range(2):
+def own_terms(sources, w_ref, acc, ops, padded, low, sub):
+    rows = ops.shape[1]
+    at = 0
+    for part, (row, shift, interleaved) in enumerate(sources):
         for r in range(rows):
-            stage(padded, part * rows + r, jnp.where(keep, own[part, r].astype(F32), 0.0), False)
-            put_warped(ops, (part, r), padded, part * rows + r, flow[0, part, 0], low, sub)
-    for r in range(rows):
-        stage(padded, 2 * rows + r, own[2, r].astype(F32), False)
-        put_plain(ops, (2, r), padded, 2 * rows + r, low)
+            stage(padded, at, row(r), interleaved)
+            if shift is None:
+                put_plain(ops, (part, r), padded, at, low)
+            else:
+                put_warped(ops, (part, r), padded, at, shift, low, sub)
+            at += 1
     first, end = local_span(rows)
     fetches = [lambda r, h, part=part: ops[part, r - RIM, h] for part in range(3)]
     acc[...] = two_row_conv(fetches, first, end - first, w_ref, (0, 1, 2))
+
+
+def start_kernel(slots, index, clip, flow, own, w_ref, acc, ops, padded):
+    lanes = own.shape[3]
+    keep = Place(index, clip, slots).keep(0)
+    clear_pads(padded)
+
+    def kept(part):
+        return lambda r: jnp.where(keep, own[part, r].astype(F32), 0.0)
+
+    own_terms(
+        (
+            (kept(0), flow[0, 0, 0], False),
+            (kept(1), flow[0, 1, 0], False),
+            (lambda r: own[2, r].astype(F32), None, False),
+        ),
+        w_ref, acc, ops, padded, lane_low(lanes), sublane(lanes),
+    )
+
+
+def ahead_kernel(
+    slots, tick, index, clip, latest, prev, feat, w_ref, acc, ops, natural, padded, plain_rows,
+    *copying,
+):
+    rows, _, lanes = latest.shape
+    place = Place(index, clip, slots)
+    keep_latest = place.keep(tick)
+    keep_earlier = keep_latest & place.keep(tick - 1)
+    shift = scalars_of(feat[0])
+    clear_pads(padded)
+    for r in range(rows):
+        plain_rows[r] = latest[r].astype(F32)
+    own_terms(
+        (
+            (lambda r: jnp.where(keep_latest, plain_rows[r], 0.0), shift[0], True),
+            (lambda r: jnp.where(keep_earlier, prev[r].astype(F32), 0.0), shift[1], tick > 1),
+            (lambda r: feat[1 + r].astype(F32), None, False),
+        ),
+        w_ref, acc, ops, padded, lane_low(lanes), sublane(lanes),
+    )
+    if copying:
+        natural_rows, sem = copying
+        rows_to_natural(natural_rows, plain_rows)
+        copy = pltpu.make_async_copy(natural_rows, natural.at[0], sem)
+        copy.start()
+        copy.wait()
+    else:
+        rows_to_natural(natural, plain_rows)
 
 
 def rows_to_natural(natural, plain_rows):
@@ -249,77 +298,8 @@
             natural[:, pair * lanes : (pair + 1) * lanes] = tile.astype(BF16)
 
 
-def ahead_kernel(
-    slots, tick, interleaved, index, clip, latest, prev, prev_one, prev_two,
-    feat, feat_above, feat_below, w_ref, acc, ops, shifts, natural,
-    padded, padded_latest, window, plain_rows, *copying,
-):
-    rows, pairs, lanes = latest.shape
-    place = Place(index, clip, slots)
-    even = place.even
-    low, sub = lane_low(lanes), sublane(lanes)
-    keep_latest = place.keep(tick)
-    keep_earlier = keep_latest & place.keep(tick - 1)
-    own_shift = scalars_of(feat[0])
-    above_shift = scalars_of(feat_above[RIM])
-    below_shift = scalars_of(feat_below[0])
-    shifts[0] = above_shift[0]
-    shifts[1] = below_shift[0]
-    clear_pads(padded)
-    clear_pads(padded_latest)
-    span = rows + 2 * RIM
-    for r in range(span):
-        if r < RIM:
-            row, ok = feat_above[r].astype(F32), place.above
-        elif r < RIM + rows:
-            row, ok = feat[1 + r - RIM].astype(F32), None
-        else:
-            row, ok = feat_below[1 + r - RIM - rows].astype(F32), place.below
-        stage(padded, r, row if ok is None else jnp.where(ok, row, 0.0), False)
-        put_plain(window, (1, r), padded, r, low)
-    for r in range(span):
-        at = span + r
-        if r < RIM:
-            row = jnp.where(even, prev_two[r], prev_one[r])
-            ok, shift = place.above & keep_earlier, above_shift[1]
-        elif r < RIM + rows:
-            row = prev[r - RIM]
-            ok, shift = keep_earlier, own_shift[1]
-        else:
-            q = r - RIM - rows
-            row = jnp.where(even, prev_one[q], prev_two[q])
-            ok, shift = place.below & keep_earlier, below_shift[1]
-        stage(padded, at, jnp.where(ok, row.astype(F32), 0.0), interleaved)
-        put_warped(window, (0, r), padded, at, shift, low, sub)
-    for r in range(rows):
-        row = latest[r].astype(F32)
-        plain_rows[r] = row
-        stage(padded_latest, r, jnp.where(keep_latest, row, 0.0), True)
-        put_warped(ops, (0, r), padded_latest, r, own_shift[0], low, sub)
-    count = (span - 2) // 2
-    first, end = local_span(rows)
-    known = [lambda r, h: window[0, r, h], lambda r, h: window[1, r, h]]
-    latest_own = [lambda r, h: ops[0, r - RIM, h]]
-    for begin, stop, fetches, layers in (
-        (0, first, known, (1, 2)),
-        (first, end, latest_own + known, (0, 1, 2)),
-        (end, count, known, (1, 2)),
-    ):
-        acc[begin * pairs : stop * pairs] = two_row_conv(
-            fetches, begin, stop - begin, w_ref, layers
-        )
-    if copying:
-        natural_rows, sem = copying
-        rows_to_natural(natural_rows, plain_rows)
-        copy = pltpu.make_async_copy(natural_rows, natural.at[0], sem)
-        copy.start()
-        copy.wait()
-    else:
-        rows_to_natural(natural, plain_rows)
-
-
 def finish_kernel(
-    slots, tick, index, clip, shifts, acc_in, ops, halo_one, halo_two, w_ref,
+    slots, tick, index, clip, acc_in, ops, halo_one, halo_two, prev, w_ref,
     latest, natural, sends, window, layers, padded, plain_rows,
 ):
     parts, rows, _, pairs, lanes = ops.shape
@@ -327,31 +307,50 @@
     even = place.even
     low, sub = lane_low(lanes), sublane(lanes)
     keep = place.keep(tick)
+    keep_both = keep if tick == 0 else keep & place.keep(tick - 1)
+
+    def above(r, one=halo_one, two=halo_two):
+        return jnp.where(even, two[r], one[r])
+
+    def below(r, one=halo_one, two=halo_two):
+        return jnp.where(even, one[r], two[r])
+
     if tick == 0:
-        marks = parts * RIM
-        above_shift = scalars_of(jnp.where(even, halo_two[marks], halo_one[marks]))
-        below_shift = scalars_of(jnp.where(even, halo_one[marks], halo_two[marks]))
+        marks = 3 * RIM
+        sides = [
+            (side, [lambda r, k=k, side=side: side(k * RIM + r) for k in range(3)],
+             scalars_of(side(marks)))
+            for side in (above, below)
+        ]
     else:
-        above_shift = (shifts[0],)
-        below_shift = (shifts[1],)
+        sides = [
+            (
+                side,
+                [
+                    lambda r, side=side: side(r),
+                    lambda r, side=side: side(r, *prev),
+                    lambda r, side=side, skip=skip: side(RIM + skip + r),
+                ],
+                scalars_of(side(mark)),
+            )
+            for side, skip, mark in ((above, 0, 2 * RIM), (below, 1, RIM))
+        ]
     clear_pads(padded)
-    order = [("above", r) for r in range(RIM)] + [("below", r) for r in range(RIM)]
     at = 0
-    for where, r in order:
-        for part in range(parts):
-            near, far = (halo_two, halo_one) if where == "above" else (halo_one, halo_two)
-            ok = place.above if where == "above" else place.below
-            shift = above_shift if where == "above" else below_shift
-            slot = r if where == "above" else RIM + r
-            row = jnp.where(even, near[part * RIM + r], far[part * RIM + r]).astype(F32)
-            if part < 2:
-                ok = ok & keep
-            stage(padded, at, jnp.where(ok, row, 0.0), tick > 0)
-            if part < 2:
-                put_warped(window, (part, slot), padded, at, shift[part], low, sub)
-            else:
-                put_plain(window, (part, slot), padded, at, low)
-            at += 1
+    for which, (side, sources, shift) in enumerate(sides):
+        inside = place.above if which == 0 else place.below
+        for r in range(RIM):
+            for part in range(parts):
+                row = sources[part](r).astype(F32)
+                ok = inside & (keep, keep_both)[part] if part < 2 else inside
+                interleaved = tick > part and part < 2
+                stage(padded, at, jnp.where(ok, row, 0.0), interleaved)
+                slot = which * RIM + r
+                if part < 2:
+                    put_warped(window, (part, slot), padded, at, shift[part], low, sub)
+                else:
+                    put_plain(window, (part, slot), padded, at, low)
+                at += 1
 
     def operand(part):
         def fetch(r, h):
@@ -397,14 +396,8 @@
         if begin != first:
             made = two_row_conv(fetches, begin, stop - begin, w_ref, join)
         for k in range(begin, stop):
-            if begin == first:
-                at = k - first if tick == 0 else k
-                both = acc_in[at * pairs : (at + 1) * pairs]
-            else:
-                both = made[(k - begin) * pairs : (k - begin + 1) * pairs]
-                if tick > 0:
-                    both = both + acc_in[k * pairs : (k + 1) * pairs]
-            emit(0, k, both)
+            source = acc_in if begin == first else made
+            emit(0, k, source[(k - begin) * pairs : (k - begin + 1) * pairs])
     for layer in range(1, 2 * RES_BLOCKS + 1):
         count -= 1
         split -= 1
@@ -430,30 +423,28 @@
         send_two[...] = latest[rows - RIM : rows]
 
 
-def pair_weights(weight):
-    before, here, after = weight[:, :, 0], weight[:, :, 1], weight[:, :, 2]
-    zero = jnp.zeros_like(here)
-    return jnp.concatenate(
-        [
-            jnp.concatenate([here, before], axis=-1),
-            jnp.concatenate([after, here], axis=-1),
-            jnp.concatenate([zero, after], axis=-1),
-            jnp.concatenate([before, zero], axis=-1),
-        ],
-        axis=2,
-    )
-
-
-def all_weights(join_weight, res_weight, channels):
-    return jnp.concatenate(
-        [
-            pair_weights(
-                join_weight.reshape(3, 3, 3, channels, channels).transpose(2, 0, 1, 3, 4)
-            ),
-            pair_weights(res_weight.reshape(2 * RES_BLOCKS, 3, 3, channels, channels)),
-        ],
-        axis=0,
-    )
+def weight_kernel(join, res, w_ref):
+    channels = join.shape[1]
+    zero = jnp.zeros((channels, channels), F32)
+
+    def fill(layer, a, taps):
+        before, here, after = taps
+        w_ref[layer, a, 0:channels] = jnp.concatenate([here, after, zero, before], axis=1).astype(
+            BF16
+        )
+        w_ref[layer, a, channels : 2 * channels] = jnp.concatenate(
+            [before, here, after, zero], axis=1
+        ).astype(BF16)
+
+    for a in range(3):
+        whole = join[a].astype(F32)
+        for part in range(3):
+            starts = [(3 * b + part) * channels for b in range(3)]
+            fill(part, a, [whole[:, at : at + channels] for at in starts])
+    for layer in range(res.shape[0]):
+        for a in range(3):
+            whole = res[layer, a].astype(F32)
+            fill(3 + layer, a, [whole[:, b * channels : (b + 1) * channels] for b in range(3)])
 
 
 def shards(features, carried, flow_shift, clip_start, join_weight, res_weight):
@@ -486,8 +477,6 @@
 
     flow = jnp.transpose(flow_shift, (1, 2, 0))
     made = rows + 2 * (RIM - 1)
-    total = made // 2 * pairs
-    span = rows + 2 * RIM
     long = pairs + 2 * PAD
     first, end = local_span(rows)
     params = pltpu.CompilerParams(vmem_limit_bytes=GRANT)
@@ -558,37 +547,35 @@
             name="start",
         )(index, clip_start, flow, own, weights)
 
-    def ahead(tick, latest, prev, prev_one, prev_two, feats):
+    def ahead(tick, latest, prev, feat):
         def kernel(*refs):
-            ahead_kernel(slots, tick, tick > 1, *refs)
+            ahead_kernel(slots, tick, *refs)
 
         whole = (TICKS,) if tick == 1 else ()
         return pl.pallas_call(
             kernel,
             out_shape=(
-                jax.ShapeDtypeStruct((total, 2 * lanes), F32),
-                jax.ShapeDtypeStruct(operands(1, rows), BF16),
-                jax.ShapeDtypeStruct((2,), jnp.int32),
+                jax.ShapeDtypeStruct(((end - first) * pairs, 2 * lanes), F32),
+                jax.ShapeDtypeStruct(operands(3, rows), BF16),
                 jax.ShapeDtypeStruct(whole + (rows, wide), BF16),
             ),
-            in_specs=[SMEM, SMEM] + [VMEM] * 8,
-            out_specs=(VMEM, VMEM, SMEM, HBM if whole else VMEM),
+            in_specs=[SMEM, SMEM] + [VMEM] * 4,
+            out_specs=(VMEM, VMEM, HBM if whole else VMEM),
             scratch_shapes=[
-                pltpu.VMEM((2 * span, long, lanes), F32),
-                pltpu.VMEM((rows, long, lanes), F32),
-                pltpu.VMEM(operands(2, span), BF16),
+                pltpu.VMEM((3 * rows, long, lanes), F32),
                 pltpu.VMEM((rows, pairs, lanes), F32),
             ]
             + ([pltpu.VMEM((rows, wide), BF16), pltpu.SemaphoreType.DMA] if whole else []),
             compiler_params=params,
-            cost_estimate=cost(made, 1),
-        )(index, clip_start, latest, prev, prev_one, prev_two, *feats, weights)
-
-    def finish(tick, shifts, acc, ops, one, two):
+            cost_estimate=cost(end - first, 3),
+        )(index, clip_start, latest, prev, feat, weights)
+
+    def finish(tick, acc, ops, one, two, prev=()):
         last = tick + 1 == TICKS
         parts = ops.shape[0]
 
-        def kernel(index, clip, shifts, acc_in, ops, one, two, w_ref, *rest):
+        def kernel(index, clip, acc_in, ops, one, two, *rest):
+            before, (w_ref, *rest) = rest[: len(prev)], rest[len(prev) :]
             if last:
                 natural, *scratch = rest
                 latest, sends = None, ()
@@ -597,7 +584,7 @@
                 natural, sends = None, (send_one, send_two)
             window, *layers, padded, plain_rows = scratch
             finish_kernel(
-                slots, tick, index, clip, shifts, acc_in, ops, one, two, w_ref,
+                slots, tick, index, clip, acc_in, ops, one, two, before, w_ref,
                 latest, natural, sends, window, layers, padded, plain_rows,
             )
 
@@ -609,7 +596,7 @@
         return pl.pallas_call(
             kernel,
             out_shape=outs,
-            in_specs=[SMEM, SMEM, SMEM] + [VMEM] * 5,
+            in_specs=[SMEM, SMEM] + [VMEM] * (5 + len(prev)),
             out_specs=(VMEM,) * len(outs),
             scratch_shapes=[pltpu.VMEM(operands(parts, 2 * RIM), BF16)]
             + [pltpu.VMEM(operands(made - 2 * layer), BF16) for layer in range(2 * RES_BLOCKS)]
@@ -619,7 +606,7 @@
             ],
             compiler_params=params,
             cost_estimate=cost(made + made // 2 * parts, 1),
-        )(index, clip_start, shifts, acc, ops, one, two, weights)
+        )(index, clip_start, acc, ops, one, two, *prev, weights)
 
     own, first_one, first_two = pack()
     later_features, first_one, first_two = lax.optimization_barrier(
@@ -631,47 +618,50 @@
     framed, own, join_weight, res_weight = lax.optimization_barrier(
         (framed, own, join_weight, res_weight)
     )
-    feats = [[] for _ in range(TICKS)]
+
+    def bring(tick):
+        return send(framed[tick - 1], shift_by(-bands * tick))
+
+    feat = bring(1)
+    weights = pl.pallas_call(
+        weight_kernel,
+        out_shape=jax.ShapeDtypeStruct((3 + 2 * RES_BLOCKS, 3, lanes, 2 * lanes), BF16),
+        in_specs=[VMEM, VMEM],
+        out_specs=VMEM,
+        compiler_params=params,
+        name="weights",
+    )(jnp.transpose(join_weight, (0, 2, 1)), jnp.transpose(res_weight, (0, 1, 3, 2)))
+    acc, ops = start(own)
+    begin_one = jnp.where(even, rows + 1 - RIM, 0)
+    begin_two = jnp.where(even, 0, rows + 1 - RIM)
+
+    def with_rim(block, frame, begin):
+        return jnp.concatenate(
+            [block, lax.dynamic_slice_in_dim(frame, begin, RIM + 1, axis=0)], axis=0
+        )
+
+    one, two = halo_one, halo_two
+    prev = own[0]
+    outs = finish(0, acc, ops, one, two)
     for tick in range(1, TICKS):
-        frame = framed[tick - 1]
-        back = -bands * tick
-        feats[tick].append(send(frame, shift_by(back)))
-        if tick == 1:
-            feats[tick].append(send(frame[rows + 1 - RIM :], shift_by(back + 1)))
-            feats[tick].append(send(frame[: RIM + 1], shift_by(back - 1)))
-    weights = all_weights(join_weight, res_weight, channels)
-    acc, ops = start(own)
-    latest, send_one, send_two = finish(
-        0, jnp.zeros((2,), jnp.int32), acc, ops, halo_one, halo_two
-    )
-    prev, prev_one, prev_two = own[0], halo_one, halo_two
-    for tick in range(1, TICKS):
-        two = send(send_two, swap_two)
-        one = send(send_one, swap_one)
-        acc, ops, shifts, natural = ahead(tick, latest, prev, prev_one, prev_two, feats[tick])
+        latest, send_one, send_two = outs
+        feat, latest, send_one, send_two = lax.optimization_barrier(
+            (feat, latest, send_one, send_two)
+        )
+        before = one, two
+        two = send(with_rim(send_two, feat, begin_two), swap_two)
+        one = send(with_rim(send_one, feat, begin_one), swap_one)
+        if tick + 1 < TICKS:
+            next_feat = bring(tick + 1)
+        acc, ops, natural = ahead(tick, latest, prev, feat)
         if tick == 1:
             result = natural
         else:
             moved = send(natural, shift_by(bands * (tick - 1)))
             result = lax.dynamic_update_slice_in_dim(result, moved[None], tick - 1, 0)
-        if tick + 1 < TICKS:
-            acc, frame = lax.optimization_barrier((acc, feats[tick + 1][0]))
-            begin_one = jnp.where(even, rows + 1 - RIM, 0)
-            begin_two = jnp.where(even, 0, rows + 1 - RIM)
-            size = RIM + 1
-            part_two = lax.dynamic_slice_in_dim(frame, begin_two, size, axis=0)
-            part_one = lax.dynamic_slice_in_dim(frame, begin_one, size, axis=0)
-            frame_two = send(part_two, swap_two)
-            frame_one = send(part_one, swap_one)
-            feats[tick + 1] = [
-                frame,
-                jnp.where(even, frame_two, frame_one),
-                jnp.where(even, frame_one, frame_two),
-            ]
-        prev, prev_one, prev_two = latest, one, two
-        outs = finish(tick, shifts, acc, ops, one, two)
-        if tick + 1 < TICKS:
-            latest, send_one, send_two = outs
+        prev = latest
+        feat = next_feat
+        outs = finish(tick, acc, ops, one, two, before)
     moved = send(outs[0], shift_by(bands * (TICKS - 1)))
     return lax.dynamic_update_slice_in_dim(result, moved[None], TICKS - 1, 0)
 
@@ -687,4 +677,6 @@
     )
     out_specs = P(None, ("groups", "rows"), None)
 
-    return jax.shard_map(shards, mesh=mesh, in_specs=in_specs, out_specs=out_specs, check_vma=False)
+    return jax.shard_map(
+        shards, mesh=mesh, in_specs=in_specs, out_specs=out_specs, check_vma=False
+    )

time: 60.1 us -> 50.4 us (0.84)
  waiting for transfers between devices: 16.8 us -> 11.7 us
  starting transfers between devices: 19.1 us -> 16.2 us
  other arithmetic: 2.32 us -> 0.08 us
  Pallas kernels: 17.8 us -> 18.6 us
    ppermute x14 -> x10, waiting for transfers between devices: 16.8 us -> 11.7 us  [send(): return lax.ppermute(block, 'rows', path)]
    ppermute x14 -> x10, starting transfers between devices: 19.1 us -> 16.2 us  [send(): return lax.ppermute(block, 'rows', path)]
    concatenate x1 -> x4, other arithmetic: 2.3 us -> 0.08 us  [with_rim(): jnp.concatenate([block, lax.dynamic_slice_in_dim(frame, begin, RIM + 1, a...]
    unnamed x8, local copies, waits for them, and re-layouts: 0.02 us -> 1.95 us
    pallas_call x5 -> x6, Pallas kernels: 13.5 us -> 14.9 us  [the longest x3 10.7 us: finish(): pl.pallas_call(kernel, out_shape=outs, in_specs=[SMEM, SMEM] + [VMEM] * (...]
    squeeze x3 -> x1, local copies, waits for them, and re-layouts: 0.8 us -> 0.01 us  [shards(): prev = own[0]]
    pallas_call x1, Pallas kernels: 1.92 us -> 1.18 us  [pack(): pl.pallas_call(kernel, out_shape=(jax.ShapeDtypeStruct((3, rows, pairs, l...]
    slice x1 -> x0, local copies, waits for them, and re-layouts: 0.7 us -> none  [shards(): feats[tick].append(send(frame[:RIM + 1], shift_by(back - 1)))]
  transfers between devices with their start and end apart: 14 -> 10, of which waited for: 5 -> 5; matrix products, arithmetic and copies ran while one was open for 8% -> 2% of each run, Pallas kernels for 23% -> 35%
where the time goes in v1:
time: 50.4 us; the launch traced here: 50.2 us
  Pallas kernels  18.6 us (37%)
  starting transfers between devices  16.2 us (32%)
  waiting for transfers between devices  11.7 us (23%)
  local copies, waits for them, and re-layouts  3.34 us (7%)
    ppermute x10, starting transfers between devices, send(): return lax.ppermute(block, 'rows', path)  16.2 us
    ppermute x10, waiting for transfers between devices, send(): return lax.ppermute(block, 'rows', path)  11.7 us
    pallas_call x3, Pallas kernels, finish(): pl.pallas_call(kernel, out_shape=outs, in_specs=[SMEM, SMEM] + [VMEM] * (...  10.7 us
    pallas_call x2, Pallas kernels, ahead(): pl.pallas_call(kernel, out_shape=(jax.ShapeDtypeStruct(((end - first) * p...  3.97 us
    unnamed x8, local copies, waits for them, and re-layouts  1.95 us
    pallas_call x1, Pallas kernels, start(): pl.pallas_call(kernel, out_shape=(jax.ShapeDtypeStruct(((end - first) * p...  1.42 us
    pallas_call x1, Pallas kernels, pack(): pl.pallas_call(kernel, out_shape=(jax.ShapeDtypeStruct((3, rows, pairs, l...  1.18 us
    pallas_call x1, Pallas kernels, frames(): pl.pallas_call(frame_kernel, out_shape=(frame,) * later, in_specs=[HBM, H...  1.06 us
  transfers between devices with their start and end apart: 10, of which 5 were waited for; matrix products, arithmetic and copies ran while one was open for 2% of the time, Pallas kernels for 35%

profile of v1, /device:TPU:0, one launch (start us, length us, event | category | flops | bytes accessed | tf_op | source)
XLA Modules:
  0.0 50.2 jit_solution(7511738771580063768)
XLA Ops:
  0.0 1.2 %pack.1 = (bf16[3,8,64,128]{3,2,1,0:T(8,128)(2,1)S(1)}, bf16[16,64,128]{2,1,0:T(8,128)(2,1)S(1)}, bf16[16,64,128]{2,1,0:T(8,128)(2,1)S(1)}) custom-call(s32[1]{0:T(128)} %bitcast.refs_0_.index, s32[1,2,3]{2,1,0:T(2,128)} %bitcast.12, bf16[2,8,8192]{2,1,0:T(8,128)(2,1)} %refs_2_.1, bf16[3,8,8192]{2,1,0:T(8,128)(2,1)} %features), custom_call_target="tpu_custom_call" | custom-call | tf_op jit(solution)/shard_map/pack/pallas_call | solution.py:499
  1.2 0.0 copy-start.2
  1.2 0.0 copy-start.3
  1.2 0.6 %collective-permute-start.1 = (bf16[16,64,128]{2,1,0:T(8,128)(2,1)S(1)}, bf16[16,64,128]{2,1,0:T(8,128)(2,1)S(1)}, u32[]{:S(2)}, u32[]{:S(2)}) collective-permute-start(bf16[16,64,128]{2,1,0:T(8,128)(2,1)S(1)} %get-tuple-element.52), channel_id=1, source_target_pairs={{0,1},{1,0},{2,3},{3,2},{4,5},{5,4},{6,7},{7,6},{8,9},{9,8},{10,11... | collective-permute-start | bytes 786440 | tf_op jit(solution)/shard_map/ppermute | solution.py:476
  1.8 5.7 %collective-permute-start.2 = (bf16[16,64,128]{2,1,0:T(8,128)(2,1)S(1)}, bf16[16,64,128]{2,1,0:T(8,128)(2,1)S(1)}, u32[]{:S(2)}, u32[]{:S(2)}) collective-permute-start(bf16[16,64,128]{2,1,0:T(8,128)(2,1)S(1)} %get-tuple-element.53), channel_id=1, source_target_pairs={{0,15},{1,2},{2,1},{3,4},{4,3},{5,6},{6,5},{7,8},{8,7},{9,10},{10,... | collective-permute-start | bytes 786440 | tf_op jit(solution)/shard_map/ppermute | solution.py:476
  7.4 1.1 %frame.1 = (bf16[10,64,128]{2,1,0:T(8,128)(2,1)S(1)}, bf16[10,64,128]{2,1,0:T(8,128)(2,1)S(1)}) custom-call(s32[1,2,3]{2,1,0:T(2,128)} %bitcast.13, bf16[3,8,8192]{2,1,0:T(8,128)(2,1)} %features), custom_call_target="tpu_custom_call" | custom-call | tf_op jit(solution)/shard_map/frame/pallas_call | solution.py:517
  8.5 0.5 collective-permute-start
  9.0 0.0 collective-permute-start.3
  9.0 0.0 copy-start
  9.0 1.0 %copy-done = bf16[4,3,192,64]{2,3,1,0:T(8,128)(2,1)S(1)} copy-done((bf16[4,3,192,64]{2,3,1,0:T(8,128)(2,1)S(1)}, bf16[4,3,192,64]{2,3,1,0:T(8,128)(2,1)}, u32[]{:S(2)}) %copy-start) | copy-done | bytes 294936
  10.0 0.0 copy-start.1
  10.0 0.9 %copy-done.1 = bf16[3,576,64]{1,2,0:T(8,128)(2,1)S(1)} copy-done((bf16[3,576,64]{1,2,0:T(8,128)(2,1)S(1)}, bf16[3,576,64]{1,2,0:T(8,128)(2,1)}, u32[]{:S(2)}) %copy-start.1) | copy-done | bytes 221208
  10.9 0.3 weights.1.refs_4_.rest_0_.refs_5_.rest_2_
  11.2 0.0 copy-done.2
  11.2 0.0 copy-done.3
  11.2 1.4 %start.1 = (f32[128,256]{1,0:T(8,128)S(1)}, bf16[3,8,2,64,128]{4,3,2,1,0:T(8,128)(2,1)S(1)}) custom-call(s32[1]{0:T(128)} %bitcast.refs_0_.index, s32[4]{0:T(128)S(1)} %copy-done.2, s32[1,2,3]{2,1,0:T(2,128)S(1)} %bitcast.14, bf16[3,8,64,128]{3,2,1,0:T(8,128)(2,1)S(1)} %get-tuple-element.47.refs_3_, ...), custom_call_target="tpu_custom_call" | custom-call | flops 100663296 | bytes 4194304 | tf_op jit(solution)/shard_map/start/pallas_call | solution.py:536
  12.7 0.0 collective-permute-done.1.one.rest_0_
  12.7 0.7 %collective-permute-done.2.two.rest_1_ = bf16[16,64,128]{2,1,0:T(8,128)(2,1)S(1)} collective-permute-done((bf16[16,64,128]{2,1,0:T(8,128)(2,1)S(1)}, bf16[16,64,128]{2,1,0:T(8,128)(2,1)S(1)}, u32[]{:S(2)}, u32[]{:S(2)}) %collective-permute-start.2) | collective-permute-done | bytes 262176 | tf_op jit(solution)/shard_map/ppermute | solution.py:476
  13.4 3.5 %shard_map.64 = (bf16[8,64,128]{2,1,0:T(8,128)(2,1)S(1)}, bf16[5,64,128]{2,1,0:T(8,128)(2,1)S(1)}, bf16[5,64,128]{2,1,0:T(8,128)(2,1)S(1)}) custom-call(s32[1]{0:T(128)} %bitcast.refs_0_.index, s32[4]{0:T(128)S(1)} %copy-done.2, f32[128,256]{1,0:T(8,128)S(1)} %get-tuple-element.50.acc_in, bf16[3,8,2,64,128]{4,3,2,1,0:T(8,128)(2,1)S(1)} %get-tuple-element.51.ops, ...), custom_call_target="tpu_custom_call" | custom-call | flops 671088640 | bytes 4194304 | tf_op jit(solution)/shard_map/pallas_call | solution.py:596
  16.9 0.0 collective-permute-done.refs_4_
  16.9 0.1 collective-permute-start.4
  17.1 4.7 %collective-permute-start.5 = (bf16[11,64,128]{2,1,0:T(8,128)(2,1)S(1)}, bf16[11,64,128]{2,1,0:T(8,128)(2,1)S(1)}, u32[]{:S(2)}, u32[]{:S(2)}) collective-permute-start(bf16[11,64,128]{2,1,0:T(8,128)(2,1)S(1)} %pad_maximum_fusion.1), channel_id=1, source_target_pairs={{0,15},{1,2},{2,1},{3,4},{4,3},{5,6},{6,5},{7,8},{8,7},{9,10},{10,... | collective-permute-start | bytes 540680 | tf_op jit(solution)/shard_map/ppermute | solution.py:476
  21.8 2.3 %shard_map.65 = (f32[128,256]{1,0:T(8,128)S(1)}, bf16[3,8,2,64,128]{4,3,2,1,0:T(8,128)(2,1)S(1)}, bf16[3,8,8192]{2,1,0:T(8,128)(2,1)}) custom-call(s32[1]{0:T(128)} %bitcast.refs_0_.index, s32[4]{0:T(128)S(1)} %copy-done.2, bf16[8,64,128]{2,1,0:T(8,128)(2,1)S(1)} %get-tuple-element.57.refs_2_.refs_3_, bf16[8,64,128]{2,1,0:T(8,128)(2,1)S(1)} %slice_bitcast_fusion.refs_3_, ...), custom_call_target="tpu_custom_call" | custom-call | flops 100663296 | bytes 4194304 | tf_op jit(solution)/shard_map/pallas_call | solution.py:555
  24.1 0.0 collective-permute-done.4.one.rest_0_
  24.1 0.9 %collective-permute-done.5.two.rest_1_ = bf16[11,64,128]{2,1,0:T(8,128)(2,1)S(1)} collective-permute-done((bf16[11,64,128]{2,1,0:T(8,128)(2,1)S(1)}, bf16[11,64,128]{2,1,0:T(8,128)(2,1)S(1)}, u32[]{:S(2)}, u32[]{:S(2)}) %collective-permute-start.5) | collective-permute-done | bytes 180256 | tf_op jit(solution)/shard_map/ppermute | solution.py:476
  25.0 3.5 %shard_map.66 = (bf16[8,64,128]{2,1,0:T(8,128)(2,1)S(1)}, bf16[5,64,128]{2,1,0:T(8,128)(2,1)S(1)}, bf16[5,64,128]{2,1,0:T(8,128)(2,1)S(1)}) custom-call(s32[1]{0:T(128)} %bitcast.refs_0_.index, s32[4]{0:T(128)S(1)} %copy-done.2, f32[128,256]{1,0:T(8,128)S(1)} %get-tuple-element.61.acc_in, bf16[3,8,2,64,128]{4,3,2,1,0:T(8,128)(2,1)S(1)} %get-tuple-element.62.ops, ...), custom_call_target="tpu_custom_call" | custom-call | flops 671088640 | bytes 4194304 | tf_op jit(solution)/shard_map/pallas_call | solution.py:596
  28.5 0.0 collective-permute-done.3.refs_4_
  28.6 0.1 collective-permute-start.7
  28.7 4.5 %collective-permute-start.8 = (bf16[11,64,128]{2,1,0:T(8,128)(2,1)S(1)}, bf16[11,64,128]{2,1,0:T(8,128)(2,1)S(1)}, u32[]{:S(2)}, u32[]{:S(2)}) collective-permute-start(bf16[11,64,128]{2,1,0:T(8,128)(2,1)S(1)} %pad_maximum_fusion.3), channel_id=1, source_target_pairs={{0,15},{1,2},{2,1},{3,4},{4,3},{5,6},{6,5},{7,8},{8,7},{9,10},{10,... | collective-permute-start | bytes 540680 | tf_op jit(solution)/shard_map/ppermute | solution.py:476
  33.2 1.7 %shard_map.67 = (f32[128,256]{1,0:T(8,128)S(1)}, bf16[3,8,2,64,128]{4,3,2,1,0:T(8,128)(2,1)S(1)}, bf16[8,8192]{1,0:T(8,128)(2,1)S(1)}) custom-call(s32[1]{0:T(128)} %bitcast.refs_0_.index, s32[4]{0:T(128)S(1)} %copy-done.2, bf16[8,64,128]{2,1,0:T(8,128)(2,1)S(1)} %get-tuple-element.68.refs_2_, bf16[8,64,128]{2,1,0:T(8,128)(2,1)S(1)} %get-tuple-element.57.refs_2_.refs_3_, ...), custom_call_target="tpu_custom_call" | custom-call | flops 100663296 | bytes 4194304 | tf_op jit(solution)/shard_map/pallas_call | solution.py:555
  34.9 0.1 collective-permute-start.6
  35.0 0.0 collective-permute-done.7.one
  35.0 2.2 %collective-permute-done.8.two = bf16[11,64,128]{2,1,0:T(8,128)(2,1)S(1)} collective-permute-done((bf16[11,64,128]{2,1,0:T(8,128)(2,1)S(1)}, bf16[11,64,128]{2,1,0:T(8,128)(2,1)S(1)}, u32[]{:S(2)}, u32[]{:S(2)}) %collective-permute-start.8) | collective-permute-done | bytes 180256 | tf_op jit(solution)/shard_map/ppermute | solution.py:476
  37.1 3.7 %shard_map.68 = bf16[8,8192]{1,0:T(8,128)(2,1)S(1)} custom-call(s32[1]{0:T(128)} %bitcast.refs_0_.index, s32[4]{0:T(128)S(1)} %copy-done.2, f32[128,256]{1,0:T(8,128)S(1)} %get-tuple-element.71.acc_in, bf16[3,8,2,64,128]{4,3,2,1,0:T(8,128)(2,1)S(1)} %get-tuple-element.72.ops, bf16[11,64,128]{2,1,0:T(8,128)(2,1)S(1)} %collective-permute-done.7.one, ...), custom_call_target="tpu_custom_call" | custom-call | flops 671088640 | bytes 4194304 | tf_op jit(solution)/shard_map/pallas_call | solution.py:596
  40.8 0.1 collective-permute-start.9
  40.9 0.8 %collective-permute-done.6 = bf16[8,8192]{1,0:T(8,128)(2,1)S(1)} collective-permute-done((bf16[8,8192]{1,0:T(8,128)(2,1)S(1)}, bf16[8,8192]{1,0:T(8,128)(2,1)S(1)}, u32[]{:S(2)}, u32[]{:S(2)}) %collective-permute-start.6) | collective-permute-done | bytes 131104 | tf_op jit(solution)/shard_map/ppermute | solution.py:476
  41.7 0.7 %bitcast_dynamic-update-slice_fusion.1 = bf16[3,8,8192]{2,1,0:T(8,128)(2,1)} fusion(bf16[3,8,8192]{2,1,0:T(8,128)(2,1)} %get-tuple-element.59, bf16[8,8192]{1,0:T(8,128)(2,1)S(1)} %collective-permute-done.6), kind=kLoop, calls=%fused_computation.5 | loop fusion | bytes 262144 | tf_op jit(solution)/shard_map/dynamic_update_slice | solution.py:661
  42.4 7.2 %collective-permute-done.9 = bf16[8,8192]{1,0:T(8,128)(2,1)S(1)} collective-permute-done((bf16[8,8192]{1,0:T(8,128)(2,1)S(1)}, bf16[8,8192]{1,0:T(8,128)(2,1)S(1)}, u32[]{:S(2)}, u32[]{:S(2)}) %collective-permute-start.9) | collective-permute-done | bytes 131104 | tf_op jit(solution)/shard_map/ppermute | solution.py:476
  49.5 0.7 %bitcast_dynamic-update-slice_fusion = bf16[3,8,8192]{2,1,0:T(8,128)(2,1)} fusion(bf16[3,8,8192]{2,1,0:T(8,128)(2,1)} %bitcast_dynamic-update-slice_fusion.1, bf16[8,8192]{1,0:T(8,128)(2,1)S(1)} %collective-permute-done.9), kind=kLoop, calls=%fused_computation.4 | loop fusion | bytes 262144 | tf_op jit(solution)/shard_map/dynamic_update_slice | solution.py:666
  (7 shorter events, 0.1 us)
Async XLA Ops:
  1.2 10.0 %copy-start.2 = (s32[4]{0:T(128)S(1)}, s32[4]{0:T(128)}, u32[]{:S(2)}) copy-start(s32[4]{0:T(128)} %clip.5) | copy-start | bytes 52
  1.2 10.0 %copy-start.3 = (s32[3,1,2]{0,2,1:T(2,128)S(1)}, s32[3,1,2]{0,2,1:T(2,128)}, u32[]{:S(2)}) copy-start(s32[3,1,2]{0,2,1:T(2,128)} %param.8) | copy-start | bytes 76
  1.2 11.4 %collective-permute-start.1 = (bf16[16,64,128]{2,1,0:T(8,128)(2,1)S(1)}, bf16[16,64,128]{2,1,0:T(8,128)(2,1)S(1)}, u32[]{:S(2)}, u32[]{:S(2)}) collective-permute-start(bf16[16,64,128]{2,1,0:T(8,128)(2,1)S(1)} %get-tuple-element.52), channel_id=1, source_target_pairs={{0,1},{1,0},{2,3},{3,2},{4,5},{5,4},{6,7},{7,6},{8,9},{9,8},{10,11... | collective-permute-start | bytes 786440 | tf_op jit(solution)/shard_map/ppermute | solution.py:476
  1.8 11.6 %collective-permute-start.2 = (bf16[16,64,128]{2,1,0:T(8,128)(2,1)S(1)}, bf16[16,64,128]{2,1,0:T(8,128)(2,1)S(1)}, u32[]{:S(2)}, u32[]{:S(2)}) collective-permute-start(bf16[16,64,128]{2,1,0:T(8,128)(2,1)S(1)} %get-tuple-element.53), channel_id=1, source_target_pairs={{0,15},{1,2},{2,1},{3,4},{4,3},{5,6},{6,5},{7,8},{8,7},{9,10},{10,... | collective-permute-start | bytes 786440 | tf_op jit(solution)/shard_map/ppermute | solution.py:476
  8.5 8.4 %collective-permute-start = (bf16[10,64,128]{2,1,0:T(8,128)(2,1)S(1)}, bf16[10,64,128]{2,1,0:T(8,128)(2,1)S(1)}, u32[]{:S(2)}, u32[]{:S(2)}) collective-permute-start(bf16[10,64,128]{2,1,0:T(8,128)(2,1)S(1)} %get-tuple-element.46), channel_id=1, source_target_pairs={{0,12},{1,13},{2,14},{3,15},{4,0},{5,1},{6,2},{7,3},{8,4},{9,5},{1... | collective-permute-start | bytes 491528 | tf_op jit(solution)/shard_map/ppermute | solution.py:476
  9.0 19.5 %collective-permute-start.3 = (bf16[10,64,128]{2,1,0:T(8,128)(2,1)S(1)}, bf16[10,64,128]{2,1,0:T(8,128)(2,1)S(1)}, u32[]{:S(2)}, u32[]{:S(2)}) collective-permute-start(bf16[10,64,128]{2,1,0:T(8,128)(2,1)S(1)} %get-tuple-element.60), channel_id=1, source_target_pairs={{0,8},{1,9},{2,10},{3,11},{4,12},{5,13},{6,14},{7,15},{8,0},{9,1},... | collective-permute-start | bytes 491528 | tf_op jit(solution)/shard_map/ppermute | solution.py:476
  9.0 1.0 %copy-start = (bf16[4,3,192,64]{2,3,1,0:T(8,128)(2,1)S(1)}, bf16[4,3,192,64]{2,3,1,0:T(8,128)(2,1)}, u32[]{:S(2)}) copy-start(bf16[4,3,192,64]{2,3,1,0:T(8,128)(2,1)} %param.11) | copy-start | bytes 884740
  10.0 0.9 %copy-start.1 = (bf16[3,576,64]{1,2,0:T(8,128)(2,1)S(1)}, bf16[3,576,64]{1,2,0:T(8,128)(2,1)}, u32[]{:S(2)}) copy-start(bf16[3,576,64]{1,2,0:T(8,128)(2,1)} %param.10) | copy-start | bytes 663556
  16.9 7.1 %collective-permute-start.4 = (bf16[11,64,128]{2,1,0:T(8,128)(2,1)S(1)}, bf16[11,64,128]{2,1,0:T(8,128)(2,1)S(1)}, u32[]{:S(2)}, u32[]{:S(2)}) collective-permute-start(bf16[11,64,128]{2,1,0:T(8,128)(2,1)S(1)} %pad_maximum_fusion), channel_id=1, source_target_pairs={{0,1},{1,0},{2,3},{3,2},{4,5},{5,4},{6,7},{7,6},{8,9},{9,8},{10,11... | collective-permute-start | bytes 540680 | tf_op jit(solution)/shard_map/ppermute | solution.py:476
  17.1 7.9 %collective-permute-start.5 = (bf16[11,64,128]{2,1,0:T(8,128)(2,1)S(1)}, bf16[11,64,128]{2,1,0:T(8,128)(2,1)S(1)}, u32[]{:S(2)}, u32[]{:S(2)}) collective-permute-start(bf16[11,64,128]{2,1,0:T(8,128)(2,1)S(1)} %pad_maximum_fusion.1), channel_id=1, source_target_pairs={{0,15},{1,2},{2,1},{3,4},{4,3},{5,6},{6,5},{7,8},{8,7},{9,10},{10,... | collective-permute-start | bytes 540680 | tf_op jit(solution)/shard_map/ppermute | solution.py:476
  28.6 6.4 %collective-permute-start.7 = (bf16[11,64,128]{2,1,0:T(8,128)(2,1)S(1)}, bf16[11,64,128]{2,1,0:T(8,128)(2,1)S(1)}, u32[]{:S(2)}, u32[]{:S(2)}) collective-permute-start(bf16[11,64,128]{2,1,0:T(8,128)(2,1)S(1)} %pad_maximum_fusion.2), channel_id=1, source_target_pairs={{0,1},{1,0},{2,3},{3,2},{4,5},{5,4},{6,7},{7,6},{8,9},{9,8},{10,11... | collective-permute-start | bytes 540680 | tf_op jit(solution)/shard_map/ppermute | solution.py:476
  28.7 8.4 %collective-permute-start.8 = (bf16[11,64,128]{2,1,0:T(8,128)(2,1)S(1)}, bf16[11,64,128]{2,1,0:T(8,128)(2,1)S(1)}, u32[]{:S(2)}, u32[]{:S(2)}) collective-permute-start(bf16[11,64,128]{2,1,0:T(8,128)(2,1)S(1)} %pad_maximum_fusion.3), channel_id=1, source_target_pairs={{0,15},{1,2},{2,1},{3,4},{4,3},{5,6},{6,5},{7,8},{8,7},{9,10},{10,... | collective-permute-start | bytes 540680 | tf_op jit(solution)/shard_map/ppermute | solution.py:476
  34.9 6.8 %collective-permute-start.6 = (bf16[8,8192]{1,0:T(8,128)(2,1)S(1)}, bf16[8,8192]{1,0:T(8,128)(2,1)S(1)}, u32[]{:S(2)}, u32[]{:S(2)}) collective-permute-start(bf16[8,8192]{1,0:T(8,128)(2,1)S(1)} %get-tuple-element.70), channel_id=1, source_target_pairs={{0,4},{1,5},{2,6},{3,7},{4,8},{5,9},{6,10},{7,11},{8,12},{9,13},{1... | collective-permute-start | bytes 393224 | tf_op jit(solution)/shard_map/ppermute | solution.py:476
  40.8 8.7 %collective-permute-start.9 = (bf16[8,8192]{1,0:T(8,128)(2,1)S(1)}, bf16[8,8192]{1,0:T(8,128)(2,1)S(1)}, u32[]{:S(2)}, u32[]{:S(2)}) collective-permute-start(bf16[8,8192]{1,0:T(8,128)(2,1)S(1)} %shard_map.68), channel_id=1, source_target_pairs={{0,8},{1,9},{2,10},{3,11},{4,12},{5,13},{6,14},{7,15},{8,0},{9,1},... | collective-permute-start | bytes 393224 | tf_op jit(solution)/shard_map/ppermute | solution.py:476

commit v2 on v1

--- a/solution.py
+++ b/solution.py
@@ -201,26 +201,22 @@
                 first[part * RIM : (part + 1) * RIM] = own[part, 0:RIM]
 
 
-def frame_kernel(flow_in, features, *rest):
-    *framed, natural, scratch, sems, flow = rest
-    _, pairs, lanes = framed[0].shape
-    rows = framed[0].shape[0] - 2
+def frame_kernel(tick, flow_in, features, frame, natural, scratch, sems, flow):
+    _, pairs, lanes = frame.shape
+    rows = frame.shape[0] - 2
     copies = [
-        pltpu.make_async_copy(features.at[later + 1], natural.at[later], sems.at[later])
-        for later in range(len(framed))
+        pltpu.make_async_copy(features.at[tick], natural, sems.at[0]),
+        pltpu.make_async_copy(flow_in, flow, sems.at[1]),
     ]
-    copies.append(pltpu.make_async_copy(flow_in, flow, sems.at[len(framed)]))
     for copy in copies:
         copy.start()
-    for later, frame in enumerate(framed):
-        copies[later].wait()
-        for r, row in enumerate(natural_to_rows(scratch.at[later], natural.at[later])):
-            frame[1 + r] = row
-    copies[-1].wait()
-    for later, frame in enumerate(framed):
-        mark = shift_row(flow, later + 1, pairs, lanes)
-        frame[0] = mark
-        frame[rows + 1] = mark
+    copies[0].wait()
+    for r, row in enumerate(natural_to_rows(scratch, natural)):
+        frame[1 + r] = row
+    copies[1].wait()
+    mark = shift_row(flow, tick, pairs, lanes)
+    frame[0] = mark
+    frame[rows + 1] = mark
 
 
 def own_terms(sources, w_ref, acc, ops, padded, low, sub):
@@ -511,22 +507,22 @@
             name="pack",
         )(index, in_hbm(flow), in_hbm(carried), in_hbm(features))
 
-    def frames(features):
-        later = TICKS - 1
-        frame = jax.ShapeDtypeStruct((rows + 2, pairs, lanes), BF16)
+    def framed(tick, features):
+        def kernel(*refs):
+            frame_kernel(tick, *refs)
+
         return pl.pallas_call(
-            frame_kernel,
-            out_shape=(frame,) * later,
+            kernel,
+            out_shape=jax.ShapeDtypeStruct((rows + 2, pairs, lanes), BF16),
             in_specs=[HBM, HBM],
-            out_specs=(VMEM,) * later,
+            out_specs=VMEM,
             scratch_shapes=[
-                pltpu.VMEM((later, rows, wide), BF16),
-                pltpu.VMEM((later, rows * (pairs + SUB), lanes), F32),
-                pltpu.SemaphoreType.DMA((later + 1,)),
+                pltpu.VMEM((rows, wide), BF16),
+                pltpu.VMEM((rows * (pairs + SUB), lanes), F32),
+                pltpu.SemaphoreType.DMA((2,)),
                 pltpu.SMEM(flow.shape, jnp.int32),
             ],
             compiler_params=params,
-            name="frame",
         )(in_hbm(flow), in_hbm(features))
 
     def start(own):
@@ -614,15 +610,15 @@
     )
     halo_two = send(first_two, swap_two)
     halo_one = send(first_one, swap_one)
-    framed = frames(later_features)
-    framed, own, join_weight, res_weight = lax.optimization_barrier(
-        (framed, own, join_weight, res_weight)
-    )
-
-    def bring(tick):
-        return send(framed[tick - 1], shift_by(-bands * tick))
-
-    feat = bring(1)
+    frame = framed(1, later_features)
+    frame, own, join_weight, res_weight = lax.optimization_barrier(
+        (frame, own, join_weight, res_weight)
+    )
+
+    def bring(tick, frame):
+        return send(frame, shift_by(-bands * tick))
+
+    feat = bring(1, frame)
     weights = pl.pallas_call(
         weight_kernel,
         out_shape=jax.ShapeDtypeStruct((3 + 2 * RES_BLOCKS, 3, lanes, 2 * lanes), BF16),
@@ -640,6 +636,8 @@
             [block, lax.dynamic_slice_in_dim(frame, begin, RIM + 1, axis=0)], axis=0
         )
 
+    last_features, acc = lax.optimization_barrier((later_features, acc))
+    second_feat = bring(2, framed(2, last_features))
     one, two = halo_one, halo_two
     prev = own[0]
     outs = finish(0, acc, ops, one, two)
@@ -651,8 +649,6 @@
         before = one, two
         two = send(with_rim(send_two, feat, begin_two), swap_two)
         one = send(with_rim(send_one, feat, begin_one), swap_one)
-        if tick + 1 < TICKS:
-            next_feat = bring(tick + 1)
         acc, ops, natural = ahead(tick, latest, prev, feat)
         if tick == 1:
             result = natural
@@ -660,7 +656,7 @@
             moved = send(natural, shift_by(bands * (tick - 1)))
             result = lax.dynamic_update_slice_in_dim(result, moved[None], tick - 1, 0)
         prev = latest
-        feat = next_feat
+        feat = second_feat
         outs = finish(tick, acc, ops, one, two, before)
     moved = send(outs[0], shift_by(bands * (TICKS - 1)))
     return lax.dynamic_update_slice_in_dim(result, moved[None], TICKS - 1, 0)

time: 50.4 us -> 49.3 us (0.978)
  Pallas kernels: 18.6 us -> 21.5 us
  local copies, waits for them, and re-layouts: 3.34 us -> 1.4 us
  waiting for transfers between devices: 11.7 us -> 9.88 us
    pallas_call x1 -> x2, Pallas kernels: 1.06 us -> 3.3 us  [framed(): pl.pallas_call(kernel, out_shape=jax.ShapeDtypeStruct((rows + 2, pairs, l...]
    unnamed x8, local copies, waits for them, and re-layouts: 1.95 us -> 0.02 us
    ppermute x10, waiting for transfers between devices: 11.7 us -> 9.88 us  [send(): return lax.ppermute(block, 'rows', path)]
    pallas_call x1, Pallas kernels: 1.18 us -> 2.02 us  [pack(): pl.pallas_call(kernel, out_shape=(jax.ShapeDtypeStruct((3, rows, pairs, l...]
  transfers between devices with their start and end apart: 10 -> 10, of which waited for: 5 -> 5; matrix products, arithmetic and copies ran while one was open for 2% -> 2% of each run, Pallas kernels for 35% -> 40%
where the time goes in v2:
time: 49.3 us; the launch traced here: 49.1 us
  Pallas kernels  21.5 us (44%)
  starting transfers between devices  16.1 us (33%)
  waiting for transfers between devices  9.88 us (20%)
  local copies, waits for them, and re-layouts  1.4 us (3%)
    ppermute x10, starting transfers between devices, send(): return lax.ppermute(block, 'rows', path)  16.1 us
    pallas_call x3, Pallas kernels, finish(): pl.pallas_call(kernel, out_shape=outs, in_specs=[SMEM, SMEM] + [VMEM] * (...  10.5 us
    ppermute x10, waiting for transfers between devices, send(): return lax.ppermute(block, 'rows', path)  9.88 us
    pallas_call x2, Pallas kernels, ahead(): pl.pallas_call(kernel, out_shape=(jax.ShapeDtypeStruct(((end - first) * p...  3.95 us
    pallas_call x2, Pallas kernels, framed(): pl.pallas_call(kernel, out_shape=jax.ShapeDtypeStruct((rows + 2, pairs, l...  3.3 us
    pallas_call x1, Pallas kernels, pack(): pl.pallas_call(kernel, out_shape=(jax.ShapeDtypeStruct((3, rows, pairs, l...  2.02 us
    pallas_call x1, Pallas kernels, start(): pl.pallas_call(kernel, out_shape=(jax.ShapeDtypeStruct(((end - first) * p...  1.39 us
  transfers between devices with their start and end apart: 10, of which 5 were waited for; matrix products, arithmetic and copies ran while one was open for 2% of the time, Pallas kernels for 40%

profile of v2, /device:TPU:0, one launch (start us, length us, event | category | flops | bytes accessed | tf_op | source)
XLA Modules:
  0.0 49.1 jit_solution(8245737562574879510)
XLA Ops:
  0.0 0.0 copy-start.1
  0.0 0.0 copy-start
  0.0 2.0 %pack.1 = (bf16[3,8,64,128]{3,2,1,0:T(8,128)(2,1)S(1)}, bf16[16,64,128]{2,1,0:T(8,128)(2,1)}, bf16[16,64,128]{2,1,0:T(8,128)(2,1)}) custom-call(s32[1]{0:T(128)} %bitcast.refs_0_.index, s32[1,2,3]{2,1,0:T(2,128)} %bitcast.12, bf16[2,8,8192]{2,1,0:T(8,128)(2,1)} %refs_2_.1, bf16[3,8,8192]{2,1,0:T(8,128)(2,1)} %refs_1_.6), custom_call_target="tpu_custom_call" | custom-call | tf_op jit(solution)/shard_map/pack/pallas_call | solution.py:495
  2.0 0.0 copy-start.2
  2.0 0.0 copy-start.3
  2.1 0.6 %collective-permute-start.1 = (bf16[16,64,128]{2,1,0:T(8,128)(2,1)}, bf16[16,64,128]{2,1,0:T(8,128)(2,1)S(1)}, u32[]{:S(2)}, u32[]{:S(2)}) collective-permute-start(bf16[16,64,128]{2,1,0:T(8,128)(2,1)} %get-tuple-element.50), channel_id=1, source_target_pairs={{0,1},{1,0},{2,3},{3,2},{4,5},{5,4},{6,7},{7,6},{8,9},{9,8},{10,11... | collective-permute-start | bytes 786440 | tf_op jit(solution)/shard_map/ppermute | solution.py:472
  2.6 5.7 %collective-permute-start.2 = (bf16[16,64,128]{2,1,0:T(8,128)(2,1)}, bf16[16,64,128]{2,1,0:T(8,128)(2,1)S(1)}, u32[]{:S(2)}, u32[]{:S(2)}) collective-permute-start(bf16[16,64,128]{2,1,0:T(8,128)(2,1)} %get-tuple-element.51), channel_id=1, source_target_pairs={{0,15},{1,2},{2,1},{3,4},{4,3},{5,6},{6,5},{7,8},{8,7},{9,10},{10,... | collective-permute-start | bytes 786440 | tf_op jit(solution)/shard_map/ppermute | solution.py:472
  8.3 1.6 %shard_map.64 = bf16[10,64,128]{2,1,0:T(8,128)(2,1)} custom-call(s32[1,2,3]{2,1,0:T(2,128)} %bitcast.13, bf16[3,8,8192]{2,1,0:T(8,128)(2,1)} %refs_1_.6), custom_call_target="tpu_custom_call" | custom-call | tf_op jit(solution)/shard_map/pallas_call | solution.py:514
  9.9 0.5 %collective-permute-start = (bf16[10,64,128]{2,1,0:T(8,128)(2,1)}, bf16[10,64,128]{2,1,0:T(8,128)(2,1)S(1)}, u32[]{:S(2)}, u32[]{:S(2)}) collective-permute-start(bf16[10,64,128]{2,1,0:T(8,128)(2,1)} %shard_map.64), channel_id=1, source_target_pairs={{0,12},{1,13},{2,14},{3,15},{4,0},{5,1},{6,2},{7,3},{8,4},{9,5},{1... | collective-permute-start | bytes 491528 | tf_op jit(solution)/shard_map/ppermute | solution.py:472
  10.4 0.0 copy-done.1
  10.4 0.0 copy-done
  10.4 0.3 weights.1.refs_4_.rest_0_.refs_5_.rest_2_
  10.7 0.0 copy-done.2
  10.7 0.0 copy-done.3
  10.7 1.4 %start.1 = (f32[128,256]{1,0:T(8,128)S(1)}, bf16[3,8,2,64,128]{4,3,2,1,0:T(8,128)(2,1)S(1)}) custom-call(s32[1]{0:T(128)} %bitcast.refs_0_.index, s32[4]{0:T(128)S(1)} %copy-done.2, s32[1,2,3]{2,1,0:T(2,128)S(1)} %bitcast.15, bf16[3,8,64,128]{3,2,1,0:T(8,128)(2,1)S(1)} %get-tuple-element.44.refs_3_, ...), custom_call_target="tpu_custom_call" | custom-call | flops 100663296 | bytes 4194304 | tf_op jit(solution)/shard_map/start/pallas_call | solution.py:532
  12.1 1.7 %shard_map.67 = bf16[10,64,128]{2,1,0:T(8,128)(2,1)} custom-call(s32[1,2,3]{2,1,0:T(2,128)} %bitcast.14, bf16[3,8,8192]{2,1,0:T(8,128)(2,1)} %refs_1_.6), custom_call_target="tpu_custom_call" | custom-call | tf_op jit(solution)/shard_map/pallas_call | solution.py:514
  13.8 0.1 collective-permute-start.3
  13.9 0.0 collective-permute-done.1.one.rest_0_
  13.9 0.0 collective-permute-done.2.two.rest_1_
  13.9 3.4 %shard_map.65 = (bf16[8,64,128]{2,1,0:T(8,128)(2,1)S(1)}, bf16[5,64,128]{2,1,0:T(8,128)(2,1)S(1)}, bf16[5,64,128]{2,1,0:T(8,128)(2,1)S(1)}) custom-call(s32[1]{0:T(128)} %bitcast.refs_0_.index, s32[4]{0:T(128)S(1)} %copy-done.2, f32[128,256]{1,0:T(8,128)S(1)} %get-tuple-element.48.acc_in, bf16[3,8,2,64,128]{4,3,2,1,0:T(8,128)(2,1)S(1)} %get-tuple-element.49.ops, ...), custom_call_target="tpu_custom_call" | custom-call | flops 671088640 | bytes 4194304 | tf_op jit(solution)/shard_map/pallas_call | solution.py:592
  17.4 0.1 collective-permute-done.refs_4_
  17.5 4.5 %collective-permute-start.5 = (bf16[11,64,128]{2,1,0:T(8,128)(2,1)S(1)}, bf16[11,64,128]{2,1,0:T(8,128)(2,1)S(1)}, u32[]{:S(2)}, u32[]{:S(2)}) collective-permute-start(bf16[11,64,128]{2,1,0:T(8,128)(2,1)S(1)} %pad_maximum_fusion.1), channel_id=1, source_target_pairs={{0,15},{1,2},{2,1},{3,4},{4,3},{5,6},{6,5},{7,8},{8,7},{9,10},{10,... | collective-permute-start | bytes 540680 | tf_op jit(solution)/shard_map/ppermute | solution.py:472
  22.0 0.1 collective-permute-start.4
  22.1 2.3 %shard_map.66 = (f32[128,256]{1,0:T(8,128)S(1)}, bf16[3,8,2,64,128]{4,3,2,1,0:T(8,128)(2,1)S(1)}, bf16[3,8,8192]{2,1,0:T(8,128)(2,1)}) custom-call(s32[1]{0:T(128)} %bitcast.refs_0_.index, s32[4]{0:T(128)S(1)} %copy-done.2, bf16[8,64,128]{2,1,0:T(8,128)(2,1)S(1)} %get-tuple-element.55.refs_2_.refs_3_, bf16[8,64,128]{2,1,0:T(8,128)(2,1)S(1)} %slice_bitcast_fusion.refs_3_, ...), custom_call_target="tpu_custom_call" | custom-call | flops 100663296 | bytes 4194304 | tf_op jit(solution)/shard_map/pallas_call | solution.py:551
  24.4 0.8 %collective-permute-done.5.two.rest_1_ = bf16[11,64,128]{2,1,0:T(8,128)(2,1)S(1)} collective-permute-done((bf16[11,64,128]{2,1,0:T(8,128)(2,1)S(1)}, bf16[11,64,128]{2,1,0:T(8,128)(2,1)S(1)}, u32[]{:S(2)}, u32[]{:S(2)}) %collective-permute-start.5) | collective-permute-done | bytes 180256 | tf_op jit(solution)/shard_map/ppermute | solution.py:472
  25.2 0.0 collective-permute-done.4.one.rest_0_
  25.2 3.5 %shard_map.68 = (bf16[8,64,128]{2,1,0:T(8,128)(2,1)S(1)}, bf16[5,64,128]{2,1,0:T(8,128)(2,1)S(1)}, bf16[5,64,128]{2,1,0:T(8,128)(2,1)S(1)}) custom-call(s32[1]{0:T(128)} %bitcast.refs_0_.index, s32[4]{0:T(128)S(1)} %copy-done.2, f32[128,256]{1,0:T(8,128)S(1)} %get-tuple-element.59.acc_in, bf16[3,8,2,64,128]{4,3,2,1,0:T(8,128)(2,1)S(1)} %get-tuple-element.60.ops, ...), custom_call_target="tpu_custom_call" | custom-call | flops 671088640 | bytes 4194304 | tf_op jit(solution)/shard_map/pallas_call | solution.py:592
  28.7 0.0 collective-permute-done.3.refs_4_
  28.8 4.5 %collective-permute-start.8 = (bf16[11,64,128]{2,1,0:T(8,128)(2,1)S(1)}, bf16[11,64,128]{2,1,0:T(8,128)(2,1)S(1)}, u32[]{:S(2)}, u32[]{:S(2)}) collective-permute-start(bf16[11,64,128]{2,1,0:T(8,128)(2,1)S(1)} %pad_maximum_fusion.3), channel_id=1, source_target_pairs={{0,15},{1,2},{2,1},{3,4},{4,3},{5,6},{6,5},{7,8},{8,7},{9,10},{10,... | collective-permute-start | bytes 540680 | tf_op jit(solution)/shard_map/ppermute | solution.py:472
  33.3 0.1 collective-permute-start.7
  33.4 1.7 %shard_map.69 = (f32[128,256]{1,0:T(8,128)S(1)}, bf16[3,8,2,64,128]{4,3,2,1,0:T(8,128)(2,1)S(1)}, bf16[8,8192]{1,0:T(8,128)(2,1)S(1)}) custom-call(s32[1]{0:T(128)} %bitcast.refs_0_.index, s32[4]{0:T(128)S(1)} %copy-done.2, bf16[8,64,128]{2,1,0:T(8,128)(2,1)S(1)} %get-tuple-element.66.refs_2_, bf16[8,64,128]{2,1,0:T(8,128)(2,1)S(1)} %get-tuple-element.55.refs_2_.refs_3_, ...), custom_call_target="tpu_custom_call" | custom-call | flops 100663296 | bytes 4194304 | tf_op jit(solution)/shard_map/pallas_call | solution.py:551
  35.1 0.1 collective-permute-start.6
  35.1 1.5 %collective-permute-done.8.two = bf16[11,64,128]{2,1,0:T(8,128)(2,1)S(1)} collective-permute-done((bf16[11,64,128]{2,1,0:T(8,128)(2,1)S(1)}, bf16[11,64,128]{2,1,0:T(8,128)(2,1)S(1)}, u32[]{:S(2)}, u32[]{:S(2)}) %collective-permute-start.8) | collective-permute-done | bytes 180256 | tf_op jit(solution)/shard_map/ppermute | solution.py:472
  36.7 0.0 collective-permute-done.7.one
  36.7 3.6 %shard_map.70 = bf16[8,8192]{1,0:T(8,128)(2,1)S(1)} custom-call(s32[1]{0:T(128)} %bitcast.refs_0_.index, s32[4]{0:T(128)S(1)} %copy-done.2, f32[128,256]{1,0:T(8,128)S(1)} %get-tuple-element.69.acc_in, bf16[3,8,2,64,128]{4,3,2,1,0:T(8,128)(2,1)S(1)} %get-tuple-element.70.ops, bf16[11,64,128]{2,1,0:T(8,128)(2,1)S(1)} %collective-permute-done.7.one, ...), custom_call_target="tpu_custom_call" | custom-call | flops 671088640 | bytes 4194304 | tf_op jit(solution)/shard_map/pallas_call | solution.py:592
  40.3 0.1 collective-permute-start.9
  40.3 2.5 %collective-permute-done.6 = bf16[8,8192]{1,0:T(8,128)(2,1)S(1)} collective-permute-done((bf16[8,8192]{1,0:T(8,128)(2,1)S(1)}, bf16[8,8192]{1,0:T(8,128)(2,1)S(1)}, u32[]{:S(2)}, u32[]{:S(2)}) %collective-permute-start.6) | collective-permute-done | bytes 131104 | tf_op jit(solution)/shard_map/ppermute | solution.py:472
  42.8 0.7 %bitcast_dynamic-update-slice_fusion.1 = bf16[3,8,8192]{2,1,0:T(8,128)(2,1)} fusion(bf16[3,8,8192]{2,1,0:T(8,128)(2,1)} %get-tuple-element.57, bf16[8,8192]{1,0:T(8,128)(2,1)S(1)} %collective-permute-done.6), kind=kLoop, calls=%fused_computation.5 | loop fusion | bytes 262144 | tf_op jit(solution)/shard_map/dynamic_update_slice | solution.py:657
  43.5 5.0 %collective-permute-done.9 = bf16[8,8192]{1,0:T(8,128)(2,1)S(1)} collective-permute-done((bf16[8,8192]{1,0:T(8,128)(2,1)S(1)}, bf16[8,8192]{1,0:T(8,128)(2,1)S(1)}, u32[]{:S(2)}, u32[]{:S(2)}) %collective-permute-start.9) | collective-permute-done | bytes 131104 | tf_op jit(solution)/shard_map/ppermute | solution.py:472
  48.4 0.7 %bitcast_dynamic-update-slice_fusion = bf16[3,8,8192]{2,1,0:T(8,128)(2,1)} fusion(bf16[3,8,8192]{2,1,0:T(8,128)(2,1)} %bitcast_dynamic-update-slice_fusion.1, bf16[8,8192]{1,0:T(8,128)(2,1)S(1)} %collective-permute-done.9), kind=kLoop, calls=%fused_computation.4 | loop fusion | bytes 262144 | tf_op jit(solution)/shard_map/dynamic_update_slice | solution.py:662
  (7 shorter events, 0.1 us)
Async XLA Ops:
  0.0 10.4 %copy-start.1 = (bf16[3,576,64]{1,2,0:T(8,128)(2,1)S(1)}, bf16[3,576,64]{1,2,0:T(8,128)(2,1)}, u32[]{:S(2)}) copy-start(bf16[3,576,64]{1,2,0:T(8,128)(2,1)} %param.10) | copy-start | bytes 663556
  0.0 10.4 %copy-start = (bf16[4,3,192,64]{2,3,1,0:T(8,128)(2,1)S(1)}, bf16[4,3,192,64]{2,3,1,0:T(8,128)(2,1)}, u32[]{:S(2)}) copy-start(bf16[4,3,192,64]{2,3,1,0:T(8,128)(2,1)} %param.11) | copy-start | bytes 884740
  2.0 8.7 %copy-start.2 = (s32[4]{0:T(128)S(1)}, s32[4]{0:T(128)}, u32[]{:S(2)}) copy-start(s32[4]{0:T(128)} %clip.5) | copy-start | bytes 52
  2.0 8.7 %copy-start.3 = (s32[3,1,2]{0,2,1:T(2,128)S(1)}, s32[3,1,2]{0,2,1:T(2,128)}, u32[]{:S(2)}) copy-start(s32[3,1,2]{0,2,1:T(2,128)} %param.8) | copy-start | bytes 76
  2.1 11.8 %collective-permute-start.1 = (bf16[16,64,128]{2,1,0:T(8,128)(2,1)}, bf16[16,64,128]{2,1,0:T(8,128)(2,1)S(1)}, u32[]{:S(2)}, u32[]{:S(2)}) collective-permute-start(bf16[16,64,128]{2,1,0:T(8,128)(2,1)} %get-tuple-element.50), channel_id=1, source_target_pairs={{0,1},{1,0},{2,3},{3,2},{4,5},{5,4},{6,7},{7,6},{8,9},{9,8},{10,11... | collective-permute-start | bytes 786440 | tf_op jit(solution)/shard_map/ppermute | solution.py:472
  2.6 11.3 %collective-permute-start.2 = (bf16[16,64,128]{2,1,0:T(8,128)(2,1)}, bf16[16,64,128]{2,1,0:T(8,128)(2,1)S(1)}, u32[]{:S(2)}, u32[]{:S(2)}) collective-permute-start(bf16[16,64,128]{2,1,0:T(8,128)(2,1)} %get-tuple-element.51), channel_id=1, source_target_pairs={{0,15},{1,2},{2,1},{3,4},{4,3},{5,6},{6,5},{7,8},{8,7},{9,10},{10,... | collective-permute-start | bytes 786440 | tf_op jit(solution)/shard_map/ppermute | solution.py:472
  9.9 7.5 %collective-permute-start = (bf16[10,64,128]{2,1,0:T(8,128)(2,1)}, bf16[10,64,128]{2,1,0:T(8,128)(2,1)S(1)}, u32[]{:S(2)}, u32[]{:S(2)}) collective-permute-start(bf16[10,64,128]{2,1,0:T(8,128)(2,1)} %shard_map.64), channel_id=1, source_target_pairs={{0,12},{1,13},{2,14},{3,15},{4,0},{5,1},{6,2},{7,3},{8,4},{9,5},{1... | collective-permute-start | bytes 491528 | tf_op jit(solution)/shard_map/ppermute | solution.py:472
  13.8 14.9 %collective-permute-start.3 = (bf16[10,64,128]{2,1,0:T(8,128)(2,1)}, bf16[10,64,128]{2,1,0:T(8,128)(2,1)S(1)}, u32[]{:S(2)}, u32[]{:S(2)}) collective-permute-start(bf16[10,64,128]{2,1,0:T(8,128)(2,1)} %shard_map.67), channel_id=1, source_target_pairs={{0,8},{1,9},{2,10},{3,11},{4,12},{5,13},{6,14},{7,15},{8,0},{9,1},... | collective-permute-start | bytes 491528 | tf_op jit(solution)/shard_map/ppermute | solution.py:472
  17.5 7.7 %collective-permute-start.5 = (bf16[11,64,128]{2,1,0:T(8,128)(2,1)S(1)}, bf16[11,64,128]{2,1,0:T(8,128)(2,1)S(1)}, u32[]{:S(2)}, u32[]{:S(2)}) collective-permute-start(bf16[11,64,128]{2,1,0:T(8,128)(2,1)S(1)} %pad_maximum_fusion.1), channel_id=1, source_target_pairs={{0,15},{1,2},{2,1},{3,4},{4,3},{5,6},{6,5},{7,8},{8,7},{9,10},{10,... | collective-permute-start | bytes 540680 | tf_op jit(solution)/shard_map/ppermute | solution.py:472
  22.0 3.2 %collective-permute-start.4 = (bf16[11,64,128]{2,1,0:T(8,128)(2,1)S(1)}, bf16[11,64,128]{2,1,0:T(8,128)(2,1)S(1)}, u32[]{:S(2)}, u32[]{:S(2)}) collective-permute-start(bf16[11,64,128]{2,1,0:T(8,128)(2,1)S(1)} %pad_maximum_fusion), channel_id=1, source_target_pairs={{0,1},{1,0},{2,3},{3,2},{4,5},{5,4},{6,7},{7,6},{8,9},{9,8},{10,11... | collective-permute-start | bytes 540680 | tf_op jit(solution)/shard_map/ppermute | solution.py:472
  28.8 7.9 %collective-permute-start.8 = (bf16[11,64,128]{2,1,0:T(8,128)(2,1)S(1)}, bf16[11,64,128]{2,1,0:T(8,128)(2,1)S(1)}, u32[]{:S(2)}, u32[]{:S(2)}) collective-permute-start(bf16[11,64,128]{2,1,0:T(8,128)(2,1)S(1)} %pad_maximum_fusion.3), channel_id=1, source_target_pairs={{0,15},{1,2},{2,1},{3,4},{4,3},{5,6},{6,5},{7,8},{8,7},{9,10},{10,... | collective-permute-start | bytes 540680 | tf_op jit(solution)/shard_map/ppermute | solution.py:472
  33.3 3.4 %collective-permute-start.7 = (bf16[11,64,128]{2,1,0:T(8,128)(2,1)S(1)}, bf16[11,64,128]{2,1,0:T(8,128)(2,1)S(1)}, u32[]{:S(2)}, u32[]{:S(2)}) collective-permute-start(bf16[11,64,128]{2,1,0:T(8,128)(2,1)S(1)} %pad_maximum_fusion.2), channel_id=1, source_target_pairs={{0,1},{1,0},{2,3},{3,2},{4,5},{5,4},{6,7},{7,6},{8,9},{9,8},{10,11... | collective-permute-start | bytes 540680 | tf_op jit(solution)/shard_map/ppermute | solution.py:472
  35.1 7.7 %collective-permute-start.6 = (bf16[8,8192]{1,0:T(8,128)(2,1)S(1)}, bf16[8,8192]{1,0:T(8,128)(2,1)S(1)}, u32[]{:S(2)}, u32[]{:S(2)}) collective-permute-start(bf16[8,8192]{1,0:T(8,128)(2,1)S(1)} %get-tuple-element.68), channel_id=1, source_target_pairs={{0,4},{1,5},{2,6},{3,7},{4,8},{5,9},{6,10},{7,11},{8,12},{9,13},{1... | collective-permute-start | bytes 393224 | tf_op jit(solution)/shard_map/ppermute | solution.py:472
  40.3 8.2 %collective-permute-start.9 = (bf16[8,8192]{1,0:T(8,128)(2,1)S(1)}, bf16[8,8192]{1,0:T(8,128)(2,1)S(1)}, u32[]{:S(2)}, u32[]{:S(2)}) collective-permute-start(bf16[8,8192]{1,0:T(8,128)(2,1)S(1)} %shard_map.70), channel_id=1, source_target_pairs={{0,8},{1,9},{2,10},{3,11},{4,12},{5,13},{6,14},{7,15},{8,0},{9,1},... | collective-permute-start | bytes 393224 | tf_op jit(solution)/shard_map/ppermute | solution.py:472

commit v3 on v2

--- a/solution.py
+++ b/solution.py
@@ -203,7 +203,6 @@
 
 def frame_kernel(tick, flow_in, features, frame, natural, scratch, sems, flow):
     _, pairs, lanes = frame.shape
-    rows = frame.shape[0] - 2
     copies = [
         pltpu.make_async_copy(features.at[tick], natural, sems.at[0]),
         pltpu.make_async_copy(flow_in, flow, sems.at[1]),
@@ -214,9 +213,7 @@
     for r, row in enumerate(natural_to_rows(scratch, natural)):
         frame[1 + r] = row
     copies[1].wait()
-    mark = shift_row(flow, tick, pairs, lanes)
-    frame[0] = mark
-    frame[rows + 1] = mark
+    frame[0] = shift_row(flow, tick, pairs, lanes)
 
 
 def own_terms(sources, w_ref, acc, ops, padded, low, sub):
@@ -298,7 +295,7 @@
     slots, tick, index, clip, acc_in, ops, halo_one, halo_two, prev, w_ref,
     latest, natural, sends, window, layers, padded, plain_rows,
 ):
-    parts, rows, _, pairs, lanes = ops.shape
+    _, rows, _, pairs, lanes = ops.shape
     place = Place(index, clip, slots)
     even = place.even
     low, sub = lane_low(lanes), sublane(lanes)
@@ -325,28 +322,12 @@
                 [
                     lambda r, side=side: side(r),
                     lambda r, side=side: side(r, *prev),
-                    lambda r, side=side, skip=skip: side(RIM + skip + r),
+                    lambda r, side=side: side(RIM + 1 + r),
                 ],
-                scalars_of(side(mark)),
+                scalars_of(side(RIM)),
             )
-            for side, skip, mark in ((above, 0, 2 * RIM), (below, 1, RIM))
+            for side in (above, below)
         ]
-    clear_pads(padded)
-    at = 0
-    for which, (side, sources, shift) in enumerate(sides):
-        inside = place.above if which == 0 else place.below
-        for r in range(RIM):
-            for part in range(parts):
-                row = sources[part](r).astype(F32)
-                ok = inside & (keep, keep_both)[part] if part < 2 else inside
-                interleaved = tick > part and part < 2
-                stage(padded, at, jnp.where(ok, row, 0.0), interleaved)
-                slot = which * RIM + r
-                if part < 2:
-                    put_warped(window, (part, slot), padded, at, shift[part], low, sub)
-                else:
-                    put_plain(window, (part, slot), padded, at, low)
-                at += 1
 
     def operand(part):
         def fetch(r, h):
@@ -361,6 +342,27 @@
     count = (rows + 2 * RIM - 2) // 2
     first, end = local_span(rows)
     split = end
+    clear_pads(padded)
+    at = 0
+    terms = {}
+    for part in (2, 0, 1):
+        for which, (side, sources, shift) in enumerate(sides):
+            ok = place.above if which == 0 else place.below
+            if part < 2:
+                ok = ok & (keep, keep_both)[part]
+            for r in range(RIM):
+                row = sources[part](r).astype(F32)
+                stage(padded, at, jnp.where(ok, row, 0.0), tick > part and part < 2)
+                slot = which * RIM + r
+                if part < 2:
+                    put_warped(window, (part, slot), padded, at, shift[part], low, sub)
+                else:
+                    put_plain(window, (part, slot), padded, at, low)
+                at += 1
+            begin, stop = ((0, first), (end, count))[which]
+            term = two_row_conv([operand(part)], begin, stop - begin, w_ref, (part,))
+            terms[begin] = terms[begin] + term if begin in terms else term
+
 
     def emit(layer, pair, both):
         margin = RIM - 1 - layer
@@ -385,14 +387,9 @@
                 else:
                     plain_rows[r] = value
 
-    fetches = [operand(part) for part in range(parts)]
-    join = tuple(range(parts))
     for begin, stop in ((0, first), (first, end), (end, count)):
-        made = None
-        if begin != first:
-            made = two_row_conv(fetches, begin, stop - begin, w_ref, join)
         for k in range(begin, stop):
-            source = acc_in if begin == first else made
+            source = acc_in if begin == first else terms[begin]
             emit(0, k, source[(k - begin) * pairs : (k - begin + 1) * pairs])
     for layer in range(1, 2 * RES_BLOCKS + 1):
         count -= 1
@@ -513,7 +510,7 @@
 
         return pl.pallas_call(
             kernel,
-            out_shape=jax.ShapeDtypeStruct((rows + 2, pairs, lanes), BF16),
+            out_shape=jax.ShapeDtypeStruct((rows + 1, pairs, lanes), BF16),
             in_specs=[HBM, HBM],
             out_specs=VMEM,
             scratch_shapes=[
@@ -628,15 +625,14 @@
         name="weights",
     )(jnp.transpose(join_weight, (0, 2, 1)), jnp.transpose(res_weight, (0, 1, 3, 2)))
     acc, ops = start(own)
-    begin_one = jnp.where(even, rows + 1 - RIM, 0)
-    begin_two = jnp.where(even, 0, rows + 1 - RIM)
+    begin_one = jnp.where(even, rows + 1 - RIM, 1)
+    begin_two = jnp.where(even, 1, rows + 1 - RIM)
 
     def with_rim(block, frame, begin):
-        return jnp.concatenate(
-            [block, lax.dynamic_slice_in_dim(frame, begin, RIM + 1, axis=0)], axis=0
-        )
-
-    last_features, acc = lax.optimization_barrier((later_features, acc))
+        rim = lax.dynamic_slice_in_dim(frame, begin, RIM, axis=0)
+        return jnp.concatenate([block, frame[0:1], rim], axis=0)
+
+    last_features = later_features
     second_feat = bring(2, framed(2, last_features))
     one, two = halo_one, halo_two
     prev = own[0]

time: 49.3 us -> 48.8 us (0.990)
  Pallas kernels: 21.5 us -> 19.5 us
  waiting for transfers between devices: 9.88 us -> 11.1 us
    pallas_call x2, Pallas kernels: 3.3 us -> 1.97 us  [framed(): pl.pallas_call(kernel, out_shape=jax.ShapeDtypeStruct((rows + 1, pairs, l...]
    ppermute x10, waiting for transfers between devices: 9.88 us -> 11.1 us  [send(): return lax.ppermute(block, 'rows', path)]
    pallas_call x1, Pallas kernels: 2.02 us -> 1.24 us  [pack(): pl.pallas_call(kernel, out_shape=(jax.ShapeDtypeStruct((3, rows, pairs, l...]
  transfers between devices with their start and end apart: 10 -> 10, of which waited for: 5 -> 5; matrix products, arithmetic and copies ran while one was open for 2% -> 2% of each run, Pallas kernels for 40% -> 37%
where the time goes in v3:
time: 48.8 us; the launch traced here: 48.7 us
  Pallas kernels  19.5 us (40%)
  starting transfers between devices  16.3 us (33%)
  waiting for transfers between devices  11.1 us (23%)
  local copies, waits for them, and re-layouts  1.41 us (3%)
    ppermute x10, starting transfers between devices, send(): return lax.ppermute(block, 'rows', path)  16.3 us
    ppermute x10, waiting for transfers between devices, send(): return lax.ppermute(block, 'rows', path)  11.1 us
    pallas_call x3, Pallas kernels, finish(): pl.pallas_call(kernel, out_shape=outs, in_specs=[SMEM, SMEM] + [VMEM] * (...  10.6 us
    pallas_call x2, Pallas kernels, ahead(): pl.pallas_call(kernel, out_shape=(jax.ShapeDtypeStruct(((end - first) * p...  3.97 us
    pallas_call x2, Pallas kernels, framed(): pl.pallas_call(kernel, out_shape=jax.ShapeDtypeStruct((rows + 1, pairs, l...  1.97 us
    pallas_call x1, Pallas kernels, start(): pl.pallas_call(kernel, out_shape=(jax.ShapeDtypeStruct(((end - first) * p...  1.42 us
    pallas_call x1, Pallas kernels, pack(): pl.pallas_call(kernel, out_shape=(jax.ShapeDtypeStruct((3, rows, pairs, l...  1.24 us
  transfers between devices with their start and end apart: 10, of which 5 were waited for; matrix products, arithmetic and copies ran while one was open for 2% of the time, Pallas kernels for 37%

profile of v3, /device:TPU:0, one launch (start us, length us, event | category | flops | bytes accessed | tf_op | source)
XLA Modules:
  0.0 48.7 jit_solution(5984980429826016932)
XLA Ops:
  0.0 0.0 copy-start.1
  0.0 0.0 copy-start
  0.0 1.2 %pack.1 = (bf16[3,8,64,128]{3,2,1,0:T(8,128)(2,1)S(1)}, bf16[16,64,128]{2,1,0:T(8,128)(2,1)S(1)}, bf16[16,64,128]{2,1,0:T(8,128)(2,1)S(1)}) custom-call(s32[1]{0:T(128)} %bitcast.refs_0_.index, s32[1,2,3]{2,1,0:T(2,128)} %bitcast.12, bf16[2,8,8192]{2,1,0:T(8,128)(2,1)} %refs_2_.1, bf16[3,8,8192]{2,1,0:T(8,128)(2,1)} %refs_1_.6), custom_call_target="tpu_custom_call" | custom-call | tf_op jit(solution)/shard_map/pack/pallas_call | solution.py:492
  1.3 0.6 %collective-permute-start.1 = (bf16[16,64,128]{2,1,0:T(8,128)(2,1)S(1)}, bf16[16,64,128]{2,1,0:T(8,128)(2,1)S(1)}, u32[]{:S(2)}, u32[]{:S(2)}) collective-permute-start(bf16[16,64,128]{2,1,0:T(8,128)(2,1)S(1)} %get-tuple-element.47), channel_id=1, source_target_pairs={{0,1},{1,0},{2,3},{3,2},{4,5},{5,4},{6,7},{7,6},{8,9},{9,8},{10,11... | collective-permute-start | bytes 786440 | tf_op jit(solution)/shard_map/ppermute | solution.py:469
  1.8 5.7 %collective-permute-start.2 = (bf16[16,64,128]{2,1,0:T(8,128)(2,1)S(1)}, bf16[16,64,128]{2,1,0:T(8,128)(2,1)S(1)}, u32[]{:S(2)}, u32[]{:S(2)}) collective-permute-start(bf16[16,64,128]{2,1,0:T(8,128)(2,1)S(1)} %get-tuple-element.48), channel_id=1, source_target_pairs={{0,15},{1,2},{2,1},{3,4},{4,3},{5,6},{6,5},{7,8},{8,7},{9,10},{10,... | collective-permute-start | bytes 786440 | tf_op jit(solution)/shard_map/ppermute | solution.py:469
  7.5 1.0 %shard_map.64 = bf16[9,64,128]{2,1,0:T(8,128)(2,1)S(1)} custom-call(s32[1,2,3]{2,1,0:T(2,128)} %bitcast.13, bf16[3,8,8192]{2,1,0:T(8,128)(2,1)} %refs_1_.6), custom_call_target="tpu_custom_call" | custom-call | tf_op jit(solution)/shard_map/pallas_call | solution.py:511
  8.5 0.0 copy-start.2
  8.5 0.0 copy-start.3
  8.5 0.5 %collective-permute-start = (bf16[9,64,128]{2,1,0:T(8,128)(2,1)S(1)}, bf16[9,64,128]{2,1,0:T(8,128)(2,1)S(1)}, u32[]{:S(2)}, u32[]{:S(2)}) collective-permute-start(bf16[9,64,128]{2,1,0:T(8,128)(2,1)S(1)} %shard_map.64), channel_id=1, source_target_pairs={{0,12},{1,13},{2,14},{3,15},{4,0},{5,1},{6,2},{7,3},{8,4},{9,5},{1... | collective-permute-start | bytes 442376 | tf_op jit(solution)/shard_map/ppermute | solution.py:469
  9.0 1.0 %shard_map.67 = bf16[9,64,128]{2,1,0:T(8,128)(2,1)S(1)} custom-call(s32[1,2,3]{2,1,0:T(2,128)} %bitcast.14, bf16[3,8,8192]{2,1,0:T(8,128)(2,1)} %refs_1_.6), custom_call_target="tpu_custom_call" | custom-call | tf_op jit(solution)/shard_map/pallas_call | solution.py:511
  10.0 0.1 collective-permute-start.3
  10.1 0.0 copy-done.1
  10.1 0.0 copy-done
  10.1 0.3 weights.1.refs_4_.rest_0_.refs_5_.rest_2_
  10.4 0.0 copy-done.2
  10.4 0.0 copy-done.3
  10.4 1.4 %start.1 = (f32[128,256]{1,0:T(8,128)S(1)}, bf16[3,8,2,64,128]{4,3,2,1,0:T(8,128)(2,1)S(1)}) custom-call(s32[1]{0:T(128)} %bitcast.refs_0_.index, s32[4]{0:T(128)S(1)} %copy-done.2, s32[1,2,3]{2,1,0:T(2,128)S(1)} %bitcast.15, bf16[3,8,64,128]{3,2,1,0:T(8,128)(2,1)S(1)} %get-tuple-element.42.refs_3_, ...), custom_call_target="tpu_custom_call" | custom-call | flops 100663296 | bytes 4194304 | tf_op jit(solution)/shard_map/start/pallas_call | solution.py:529
  11.8 0.0 collective-permute-done.1.one.rest_0_
  11.8 1.6 %collective-permute-done.2.two.rest_1_ = bf16[16,64,128]{2,1,0:T(8,128)(2,1)S(1)} collective-permute-done((bf16[16,64,128]{2,1,0:T(8,128)(2,1)S(1)}, bf16[16,64,128]{2,1,0:T(8,128)(2,1)S(1)}, u32[]{:S(2)}, u32[]{:S(2)}) %collective-permute-start.2) | collective-permute-done | bytes 262176 | tf_op jit(solution)/shard_map/ppermute | solution.py:469
  13.5 3.5 %shard_map.65 = (bf16[8,64,128]{2,1,0:T(8,128)(2,1)S(1)}, bf16[5,64,128]{2,1,0:T(8,128)(2,1)S(1)}, bf16[5,64,128]{2,1,0:T(8,128)(2,1)S(1)}) custom-call(s32[1]{0:T(128)} %bitcast.refs_0_.index, s32[4]{0:T(128)S(1)} %copy-done.2, f32[128,256]{1,0:T(8,128)S(1)} %get-tuple-element.45.acc_in, bf16[3,8,2,64,128]{4,3,2,1,0:T(8,128)(2,1)S(1)} %get-tuple-element.46.ops, ...), custom_call_target="tpu_custom_call" | custom-call | flops 671088640 | bytes 4194304 | tf_op jit(solution)/shard_map/pallas_call | solution.py:589
  17.0 0.0 collective-permute-done.refs_4_
  17.0 0.1 collective-permute-start.4
  17.1 4.7 %collective-permute-start.5 = (bf16[11,64,128]{2,1,0:T(8,128)(2,1)S(1)}, bf16[11,64,128]{2,1,0:T(8,128)(2,1)S(1)}, u32[]{:S(2)}, u32[]{:S(2)}) collective-permute-start(bf16[11,64,128]{2,1,0:T(8,128)(2,1)S(1)} %get-tuple-element.75), channel_id=1, source_target_pairs={{0,15},{1,2},{2,1},{3,4},{4,3},{5,6},{6,5},{7,8},{8,7},{9,10},{10,... | collective-permute-start | bytes 540680 | tf_op jit(solution)/shard_map/ppermute | solution.py:469
  21.9 2.3 %shard_map.66 = (f32[128,256]{1,0:T(8,128)S(1)}, bf16[3,8,2,64,128]{4,3,2,1,0:T(8,128)(2,1)S(1)}, bf16[3,8,8192]{2,1,0:T(8,128)(2,1)}) custom-call(s32[1]{0:T(128)} %bitcast.refs_0_.index, s32[4]{0:T(128)S(1)} %copy-done.2, bf16[8,64,128]{2,1,0:T(8,128)(2,1)S(1)} %get-tuple-element.52.refs_2_.refs_3_, bf16[8,64,128]{2,1,0:T(8,128)(2,1)S(1)} %slice_bitcast_fusion.refs_3_, ...), custom_call_target="tpu_custom_call" | custom-call | flops 100663296 | bytes 4194304 | tf_op jit(solution)/shard_map/pallas_call | solution.py:548
  24.1 0.0 collective-permute-done.4.one.rest_0_
  24.2 0.9 %collective-permute-done.5.two.rest_1_ = bf16[11,64,128]{2,1,0:T(8,128)(2,1)S(1)} collective-permute-done((bf16[11,64,128]{2,1,0:T(8,128)(2,1)S(1)}, bf16[11,64,128]{2,1,0:T(8,128)(2,1)S(1)}, u32[]{:S(2)}, u32[]{:S(2)}) %collective-permute-start.5) | collective-permute-done | bytes 180256 | tf_op jit(solution)/shard_map/ppermute | solution.py:469
  25.0 3.5 %shard_map.68 = (bf16[8,64,128]{2,1,0:T(8,128)(2,1)S(1)}, bf16[5,64,128]{2,1,0:T(8,128)(2,1)S(1)}, bf16[5,64,128]{2,1,0:T(8,128)(2,1)S(1)}) custom-call(s32[1]{0:T(128)} %bitcast.refs_0_.index, s32[4]{0:T(128)S(1)} %copy-done.2, f32[128,256]{1,0:T(8,128)S(1)} %get-tuple-element.55.acc_in, bf16[3,8,2,64,128]{4,3,2,1,0:T(8,128)(2,1)S(1)} %get-tuple-element.56.ops, ...), custom_call_target="tpu_custom_call" | custom-call | flops 671088640 | bytes 4194304 | tf_op jit(solution)/shard_map/pallas_call | solution.py:589
  28.5 0.0 collective-permute-done.3.refs_4_
  28.6 0.1 collective-permute-start.7
  28.7 4.5 %collective-permute-start.8 = (bf16[11,64,128]{2,1,0:T(8,128)(2,1)S(1)}, bf16[11,64,128]{2,1,0:T(8,128)(2,1)S(1)}, u32[]{:S(2)}, u32[]{:S(2)}) collective-permute-start(bf16[11,64,128]{2,1,0:T(8,128)(2,1)S(1)} %get-tuple-element.73), channel_id=1, source_target_pairs={{0,15},{1,2},{2,1},{3,4},{4,3},{5,6},{6,5},{7,8},{8,7},{9,10},{10,... | collective-permute-start | bytes 540680 | tf_op jit(solution)/shard_map/ppermute | solution.py:469
  33.2 1.7 %shard_map.69 = (f32[128,256]{1,0:T(8,128)S(1)}, bf16[3,8,2,64,128]{4,3,2,1,0:T(8,128)(2,1)S(1)}, bf16[8,8192]{1,0:T(8,128)(2,1)S(1)}) custom-call(s32[1]{0:T(128)} %bitcast.refs_0_.index, s32[4]{0:T(128)S(1)} %copy-done.2, bf16[8,64,128]{2,1,0:T(8,128)(2,1)S(1)} %get-tuple-element.62.refs_2_, bf16[8,64,128]{2,1,0:T(8,128)(2,1)S(1)} %get-tuple-element.52.refs_2_.refs_3_, ...), custom_call_target="tpu_custom_call" | custom-call | flops 100663296 | bytes 4194304 | tf_op jit(solution)/shard_map/pallas_call | solution.py:548
  34.9 0.1 collective-permute-start.6
  35.0 0.0 collective-permute-done.7.one
  35.0 1.4 %collective-permute-done.8.two = bf16[11,64,128]{2,1,0:T(8,128)(2,1)S(1)} collective-permute-done((bf16[11,64,128]{2,1,0:T(8,128)(2,1)S(1)}, bf16[11,64,128]{2,1,0:T(8,128)(2,1)S(1)}, u32[]{:S(2)}, u32[]{:S(2)}) %collective-permute-start.8) | collective-permute-done | bytes 180256 | tf_op jit(solution)/shard_map/ppermute | solution.py:469
  36.4 3.6 %shard_map.70 = bf16[8,8192]{1,0:T(8,128)(2,1)S(1)} custom-call(s32[1]{0:T(128)} %bitcast.refs_0_.index, s32[4]{0:T(128)S(1)} %copy-done.2, f32[128,256]{1,0:T(8,128)S(1)} %get-tuple-element.65.acc_in, bf16[3,8,2,64,128]{4,3,2,1,0:T(8,128)(2,1)S(1)} %get-tuple-element.66.ops, bf16[11,64,128]{2,1,0:T(8,128)(2,1)S(1)} %collective-permute-done.7.one, ...), custom_call_target="tpu_custom_call" | custom-call | flops 671088640 | bytes 4194304 | tf_op jit(solution)/shard_map/pallas_call | solution.py:589
  40.1 0.1 collective-permute-start.9
  40.1 1.7 %collective-permute-done.6 = bf16[8,8192]{1,0:T(8,128)(2,1)S(1)} collective-permute-done((bf16[8,8192]{1,0:T(8,128)(2,1)S(1)}, bf16[8,8192]{1,0:T(8,128)(2,1)S(1)}, u32[]{:S(2)}, u32[]{:S(2)}) %collective-permute-start.6) | collective-permute-done | bytes 131104 | tf_op jit(solution)/shard_map/ppermute | solution.py:469
  41.8 0.7 %bitcast_dynamic-update-slice_fusion.1 = bf16[3,8,8192]{2,1,0:T(8,128)(2,1)} fusion(bf16[3,8,8192]{2,1,0:T(8,128)(2,1)} %get-tuple-element.54, bf16[8,8192]{1,0:T(8,128)(2,1)S(1)} %collective-permute-done.6), kind=kLoop, calls=%fused_computation.9 | loop fusion | bytes 262144 | tf_op jit(solution)/shard_map/dynamic_update_slice | solution.py:653
  42.4 5.5 %collective-permute-done.9 = bf16[8,8192]{1,0:T(8,128)(2,1)S(1)} collective-permute-done((bf16[8,8192]{1,0:T(8,128)(2,1)S(1)}, bf16[8,8192]{1,0:T(8,128)(2,1)S(1)}, u32[]{:S(2)}, u32[]{:S(2)}) %collective-permute-start.9) | collective-permute-done | bytes 131104 | tf_op jit(solution)/shard_map/ppermute | solution.py:469
  48.0 0.7 %bitcast_dynamic-update-slice_fusion = bf16[3,8,8192]{2,1,0:T(8,128)(2,1)} fusion(bf16[3,8,8192]{2,1,0:T(8,128)(2,1)} %bitcast_dynamic-update-slice_fusion.1, bf16[8,8192]{1,0:T(8,128)(2,1)S(1)} %collective-permute-done.9), kind=kLoop, calls=%fused_computation.8 | loop fusion | bytes 262144 | tf_op jit(solution)/shard_map/dynamic_update_slice | solution.py:658
  (7 shorter events, 0.1 us)
Async XLA Ops:
  0.0 10.1 %copy-start.1 = (bf16[3,576,64]{1,2,0:T(8,128)(2,1)S(1)}, bf16[3,576,64]{1,2,0:T(8,128)(2,1)}, u32[]{:S(2)}) copy-start(bf16[3,576,64]{1,2,0:T(8,128)(2,1)} %param.10) | copy-start | bytes 663556
  0.0 10.1 %copy-start = (bf16[4,3,192,64]{2,3,1,0:T(8,128)(2,1)S(1)}, bf16[4,3,192,64]{2,3,1,0:T(8,128)(2,1)}, u32[]{:S(2)}) copy-start(bf16[4,3,192,64]{2,3,1,0:T(8,128)(2,1)} %param.11) | copy-start | bytes 884740
  1.3 10.6 %collective-permute-start.1 = (bf16[16,64,128]{2,1,0:T(8,128)(2,1)S(1)}, bf16[16,64,128]{2,1,0:T(8,128)(2,1)S(1)}, u32[]{:S(2)}, u32[]{:S(2)}) collective-permute-start(bf16[16,64,128]{2,1,0:T(8,128)(2,1)S(1)} %get-tuple-element.47), channel_id=1, source_target_pairs={{0,1},{1,0},{2,3},{3,2},{4,5},{5,4},{6,7},{7,6},{8,9},{9,8},{10,11... | collective-permute-start | bytes 786440 | tf_op jit(solution)/shard_map/ppermute | solution.py:469
  1.8 11.7 %collective-permute-start.2 = (bf16[16,64,128]{2,1,0:T(8,128)(2,1)S(1)}, bf16[16,64,128]{2,1,0:T(8,128)(2,1)S(1)}, u32[]{:S(2)}, u32[]{:S(2)}) collective-permute-start(bf16[16,64,128]{2,1,0:T(8,128)(2,1)S(1)} %get-tuple-element.48), channel_id=1, source_target_pairs={{0,15},{1,2},{2,1},{3,4},{4,3},{5,6},{6,5},{7,8},{8,7},{9,10},{10,... | collective-permute-start | bytes 786440 | tf_op jit(solution)/shard_map/ppermute | solution.py:469
  8.5 1.9 %copy-start.2 = (s32[4]{0:T(128)S(1)}, s32[4]{0:T(128)}, u32[]{:S(2)}) copy-start(s32[4]{0:T(128)} %clip.5) | copy-start | bytes 52
  8.5 1.9 %copy-start.3 = (s32[3,1,2]{0,2,1:T(2,128)S(1)}, s32[3,1,2]{0,2,1:T(2,128)}, u32[]{:S(2)}) copy-start(s32[3,1,2]{0,2,1:T(2,128)} %param.8) | copy-start | bytes 76
  8.5 8.5 %collective-permute-start = (bf16[9,64,128]{2,1,0:T(8,128)(2,1)S(1)}, bf16[9,64,128]{2,1,0:T(8,128)(2,1)S(1)}, u32[]{:S(2)}, u32[]{:S(2)}) collective-permute-start(bf16[9,64,128]{2,1,0:T(8,128)(2,1)S(1)} %shard_map.64), channel_id=1, source_target_pairs={{0,12},{1,13},{2,14},{3,15},{4,0},{5,1},{6,2},{7,3},{8,4},{9,5},{1... | collective-permute-start | bytes 442376 | tf_op jit(solution)/shard_map/ppermute | solution.py:469
  10.0 18.5 %collective-permute-start.3 = (bf16[9,64,128]{2,1,0:T(8,128)(2,1)S(1)}, bf16[9,64,128]{2,1,0:T(8,128)(2,1)S(1)}, u32[]{:S(2)}, u32[]{:S(2)}) collective-permute-start(bf16[9,64,128]{2,1,0:T(8,128)(2,1)S(1)} %shard_map.67), channel_id=1, source_target_pairs={{0,8},{1,9},{2,10},{3,11},{4,12},{5,13},{6,14},{7,15},{8,0},{9,1},... | collective-permute-start | bytes 442376 | tf_op jit(solution)/shard_map/ppermute | solution.py:469
  17.0 7.1 %collective-permute-start.4 = (bf16[11,64,128]{2,1,0:T(8,128)(2,1)S(1)}, bf16[11,64,128]{2,1,0:T(8,128)(2,1)S(1)}, u32[]{:S(2)}, u32[]{:S(2)}) collective-permute-start(bf16[11,64,128]{2,1,0:T(8,128)(2,1)S(1)} %get-tuple-element.76), channel_id=1, source_target_pairs={{0,1},{1,0},{2,3},{3,2},{4,5},{5,4},{6,7},{7,6},{8,9},{9,8},{10,11... | collective-permute-start | bytes 540680 | tf_op jit(solution)/shard_map/ppermute | solution.py:469
  17.1 7.9 %collective-permute-start.5 = (bf16[11,64,128]{2,1,0:T(8,128)(2,1)S(1)}, bf16[11,64,128]{2,1,0:T(8,128)(2,1)S(1)}, u32[]{:S(2)}, u32[]{:S(2)}) collective-permute-start(bf16[11,64,128]{2,1,0:T(8,128)(2,1)S(1)} %get-tuple-element.75), channel_id=1, source_target_pairs={{0,15},{1,2},{2,1},{3,4},{4,3},{5,6},{6,5},{7,8},{8,7},{9,10},{10,... | collective-permute-start | bytes 540680 | tf_op jit(solution)/shard_map/ppermute | solution.py:469
  28.6 6.4 %collective-permute-start.7 = (bf16[11,64,128]{2,1,0:T(8,128)(2,1)S(1)}, bf16[11,64,128]{2,1,0:T(8,128)(2,1)S(1)}, u32[]{:S(2)}, u32[]{:S(2)}) collective-permute-start(bf16[11,64,128]{2,1,0:T(8,128)(2,1)S(1)} %get-tuple-element.74), channel_id=1, source_target_pairs={{0,1},{1,0},{2,3},{3,2},{4,5},{5,4},{6,7},{7,6},{8,9},{9,8},{10,11... | collective-permute-start | bytes 540680 | tf_op jit(solution)/shard_map/ppermute | solution.py:469
  28.7 7.7 %collective-permute-start.8 = (bf16[11,64,128]{2,1,0:T(8,128)(2,1)S(1)}, bf16[11,64,128]{2,1,0:T(8,128)(2,1)S(1)}, u32[]{:S(2)}, u32[]{:S(2)}) collective-permute-start(bf16[11,64,128]{2,1,0:T(8,128)(2,1)S(1)} %get-tuple-element.73), channel_id=1, source_target_pairs={{0,15},{1,2},{2,1},{3,4},{4,3},{5,6},{6,5},{7,8},{8,7},{9,10},{10,... | collective-permute-start | bytes 540680 | tf_op jit(solution)/shard_map/ppermute | solution.py:469
  34.9 6.9 %collective-permute-start.6 = (bf16[8,8192]{1,0:T(8,128)(2,1)S(1)}, bf16[8,8192]{1,0:T(8,128)(2,1)S(1)}, u32[]{:S(2)}, u32[]{:S(2)}) collective-permute-start(bf16[8,8192]{1,0:T(8,128)(2,1)S(1)} %get-tuple-element.64), channel_id=1, source_target_pairs={{0,4},{1,5},{2,6},{3,7},{4,8},{5,9},{6,10},{7,11},{8,12},{9,13},{1... | collective-permute-start | bytes 393224 | tf_op jit(solution)/shard_map/ppermute | solution.py:469
  40.1 7.9 %collective-permute-start.9 = (bf16[8,8192]{1,0:T(8,128)(2,1)S(1)}, bf16[8,8192]{1,0:T(8,128)(2,1)S(1)}, u32[]{:S(2)}, u32[]{:S(2)}) collective-permute-start(bf16[8,8192]{1,0:T(8,128)(2,1)S(1)} %shard_map.70), channel_id=1, source_target_pairs={{0,8},{1,9},{2,10},{3,11},{4,12},{5,13},{6,14},{7,15},{8,0},{9,1},... | collective-permute-start | bytes 393224 | tf_op jit(solution)/shard_map/ppermute | solution.py:469

commit v4 on v3

--- a/solution.py
+++ b/solution.py
@@ -86,15 +86,13 @@
 
 
 def two_row_weight(w_ref, layers):
-    zero = jnp.zeros(w_ref.shape[2:], BF16)
-    upper, lower = [], []
+    rows = []
     for layer in layers:
+        zero = jnp.zeros(w_ref.shape[2:], BF16)
         w = [w_ref[layer, a] for a in range(3)]
-        upper += w + [zero]
-        lower += [zero] + w
-    return jnp.concatenate(
-        [jnp.concatenate(upper, axis=1), jnp.concatenate(lower, axis=1)], axis=0
-    )
+        for pair in ((w[0], zero), (w[1], w[0]), (w[2], w[1]), (zero, w[2])):
+            rows.append(jnp.concatenate(pair, axis=1))
+    return jnp.concatenate(rows, axis=0)
 
 
 def two_row_conv(fetches, first, count, w_ref, layers):
@@ -110,7 +108,7 @@
     return lax.dot_general(
         jnp.concatenate(columns, axis=1),
         two_row_weight(w_ref, layers),
-        (((1,), (1,)), ((), ())),
+        (((1,), (0,)), ((), ())),
         preferred_element_type=F32,
     )
 
@@ -341,11 +339,11 @@
 
     count = (rows + 2 * RIM - 2) // 2
     first, end = local_span(rows)
-    split = end
+    split = end + 1
     clear_pads(padded)
     at = 0
     terms = {}
-    for part in (2, 0, 1):
+    for part in (2, 1, 0):
         for which, (side, sources, shift) in enumerate(sides):
             ok = place.above if which == 0 else place.below
             if part < 2:
@@ -422,12 +420,9 @@
 
     def fill(layer, a, taps):
         before, here, after = taps
-        w_ref[layer, a, 0:channels] = jnp.concatenate([here, after, zero, before], axis=1).astype(
-            BF16
-        )
-        w_ref[layer, a, channels : 2 * channels] = jnp.concatenate(
-            [before, here, after, zero], axis=1
-        ).astype(BF16)
+        left = jnp.concatenate([here, after, zero, before], axis=1)
+        right = jnp.concatenate([before, here, after, zero], axis=1)
+        w_ref[layer, a] = jnp.concatenate([left, right], axis=0).T.astype(BF16)
 
     for a in range(3):
         whole = join[a].astype(F32)
@@ -618,7 +613,7 @@
     feat = bring(1, frame)
     weights = pl.pallas_call(
         weight_kernel,
-        out_shape=jax.ShapeDtypeStruct((3 + 2 * RES_BLOCKS, 3, lanes, 2 * lanes), BF16),
+        out_shape=jax.ShapeDtypeStruct((3 + 2 * RES_BLOCKS, 3, 2 * lanes, lanes), BF16),
         in_specs=[VMEM, VMEM],
         out_specs=VMEM,
         compiler_params=params,

time: 48.8 us -> 47.8 us (0.980)
  Pallas kernels: 19.5 us -> 18.3 us
    pallas_call x3, Pallas kernels: 10.6 us -> 9.48 us  [finish(): pl.pallas_call(kernel, out_shape=outs, in_specs=[SMEM, SMEM] + [VMEM] * (...]
  transfers between devices with their start and end apart: 10 -> 10, of which waited for: 5 -> 5; matrix products, arithmetic and copies ran while one was open for 2% -> 2% of each run, Pallas kernels for 37% -> 36%
where the time goes in v4:
time: 47.8 us; the launch traced here: 47.6 us
  Pallas kernels  18.3 us (38%)
  starting transfers between devices  16.3 us (34%)
  waiting for transfers between devices  11.3 us (24%)
  local copies, waits for them, and re-layouts  1.41 us (3%)
    ppermute x10, starting transfers between devices, send(): return lax.ppermute(block, 'rows', path)  16.3 us
    ppermute x10, waiting for transfers between devices, send(): return lax.ppermute(block, 'rows', path)  11.3 us
    pallas_call x3, Pallas kernels, finish(): pl.pallas_call(kernel, out_shape=outs, in_specs=[SMEM, SMEM] + [VMEM] * (...  9.48 us
    pallas_call x2, Pallas kernels, ahead(): pl.pallas_call(kernel, out_shape=(jax.ShapeDtypeStruct(((end - first) * p...  3.67 us
    pallas_call x2, Pallas kernels, framed(): pl.pallas_call(kernel, out_shape=jax.ShapeDtypeStruct((rows + 1, pairs, l...  1.97 us
    pallas_call x1, Pallas kernels, start(): pl.pallas_call(kernel, out_shape=(jax.ShapeDtypeStruct(((end - first) * p...  1.28 us
    pallas_call x1, Pallas kernels, pack(): pl.pallas_call(kernel, out_shape=(jax.ShapeDtypeStruct((3, rows, pairs, l...  1.24 us
  transfers between devices with their start and end apart: 10, of which 5 were waited for; matrix products, arithmetic and copies ran while one was open for 2% of the time, Pallas kernels for 36%

profile of v4, /device:TPU:0, one launch (start us, length us, event | category | flops | bytes accessed | tf_op | source)
XLA Modules:
  0.0 47.6 jit_solution(4582585056354441124)
XLA Ops:
  0.0 0.0 copy-start.1
  0.0 0.0 copy-start
  0.0 1.2 %pack.1 = (bf16[3,8,64,128]{3,2,1,0:T(8,128)(2,1)S(1)}, bf16[16,64,128]{2,1,0:T(8,128)(2,1)S(1)}, bf16[16,64,128]{2,1,0:T(8,128)(2,1)S(1)}) custom-call(s32[1]{0:T(128)} %bitcast.refs_0_.index, s32[1,2,3]{2,1,0:T(2,128)} %bitcast.12, bf16[2,8,8192]{2,1,0:T(8,128)(2,1)} %refs_2_.1, bf16[3,8,8192]{2,1,0:T(8,128)(2,1)} %refs_1_.6), custom_call_target="tpu_custom_call" | custom-call | tf_op jit(solution)/shard_map/pack/pallas_call | solution.py:487
  1.3 0.6 %collective-permute-start.1 = (bf16[16,64,128]{2,1,0:T(8,128)(2,1)S(1)}, bf16[16,64,128]{2,1,0:T(8,128)(2,1)S(1)}, u32[]{:S(2)}, u32[]{:S(2)}) collective-permute-start(bf16[16,64,128]{2,1,0:T(8,128)(2,1)S(1)} %get-tuple-element.47), channel_id=1, source_target_pairs={{0,1},{1,0},{2,3},{3,2},{4,5},{5,4},{6,7},{7,6},{8,9},{9,8},{10,11... | collective-permute-start | bytes 786440 | tf_op jit(solution)/shard_map/ppermute | solution.py:464
  1.8 5.7 %collective-permute-start.2 = (bf16[16,64,128]{2,1,0:T(8,128)(2,1)S(1)}, bf16[16,64,128]{2,1,0:T(8,128)(2,1)S(1)}, u32[]{:S(2)}, u32[]{:S(2)}) collective-permute-start(bf16[16,64,128]{2,1,0:T(8,128)(2,1)S(1)} %get-tuple-element.48), channel_id=1, source_target_pairs={{0,15},{1,2},{2,1},{3,4},{4,3},{5,6},{6,5},{7,8},{8,7},{9,10},{10,... | collective-permute-start | bytes 786440 | tf_op jit(solution)/shard_map/ppermute | solution.py:464
  7.5 1.0 %shard_map.64 = bf16[9,64,128]{2,1,0:T(8,128)(2,1)S(1)} custom-call(s32[1,2,3]{2,1,0:T(2,128)} %bitcast.13, bf16[3,8,8192]{2,1,0:T(8,128)(2,1)} %refs_1_.6), custom_call_target="tpu_custom_call" | custom-call | tf_op jit(solution)/shard_map/pallas_call | solution.py:506
  8.5 0.0 copy-start.2
  8.5 0.0 copy-start.3
  8.5 0.5 %collective-permute-start = (bf16[9,64,128]{2,1,0:T(8,128)(2,1)S(1)}, bf16[9,64,128]{2,1,0:T(8,128)(2,1)S(1)}, u32[]{:S(2)}, u32[]{:S(2)}) collective-permute-start(bf16[9,64,128]{2,1,0:T(8,128)(2,1)S(1)} %shard_map.64), channel_id=1, source_target_pairs={{0,12},{1,13},{2,14},{3,15},{4,0},{5,1},{6,2},{7,3},{8,4},{9,5},{1... | collective-permute-start | bytes 442376 | tf_op jit(solution)/shard_map/ppermute | solution.py:464
  9.0 1.0 %shard_map.67 = bf16[9,64,128]{2,1,0:T(8,128)(2,1)S(1)} custom-call(s32[1,2,3]{2,1,0:T(2,128)} %bitcast.14, bf16[3,8,8192]{2,1,0:T(8,128)(2,1)} %refs_1_.6), custom_call_target="tpu_custom_call" | custom-call | tf_op jit(solution)/shard_map/pallas_call | solution.py:506
  10.0 0.1 collective-permute-start.3
  10.1 0.0 copy-done.1
  10.1 0.0 copy-done
  10.1 0.6 %weights.1.refs_4_.rest_0_.refs_5_.rest_2_ = bf16[7,3,256,128]{3,2,1,0:T(8,128)(2,1)S(1)} custom-call(bf16[3,64,576]{2,1,0:T(8,128)(2,1)S(1)} %bitcast.11, bf16[4,3,64,192]{3,2,1,0:T(8,128)(2,1)S(1)} %bitcast.10), custom_call_target="tpu_custom_call" | custom-call | tf_op jit(solution)/shard_map/weights/pallas_call | solution.py:614
  10.7 0.0 copy-done.2
  10.7 0.0 copy-done.3
  10.8 1.3 %start.1 = (f32[128,256]{1,0:T(8,128)S(1)}, bf16[3,8,2,64,128]{4,3,2,1,0:T(8,128)(2,1)S(1)}) custom-call(s32[1]{0:T(128)} %bitcast.refs_0_.index, s32[4]{0:T(128)S(1)} %copy-done.2, s32[1,2,3]{2,1,0:T(2,128)S(1)} %bitcast.15, bf16[3,8,64,128]{3,2,1,0:T(8,128)(2,1)S(1)} %get-tuple-element.42.refs_3_, ...), custom_call_target="tpu_custom_call" | custom-call | flops 100663296 | bytes 4194304 | tf_op jit(solution)/shard_map/start/pallas_call | solution.py:524
  12.0 0.0 collective-permute-done.1.one.rest_0_
  12.0 1.4 %collective-permute-done.2.two.rest_1_ = bf16[16,64,128]{2,1,0:T(8,128)(2,1)S(1)} collective-permute-done((bf16[16,64,128]{2,1,0:T(8,128)(2,1)S(1)}, bf16[16,64,128]{2,1,0:T(8,128)(2,1)S(1)}, u32[]{:S(2)}, u32[]{:S(2)}) %collective-permute-start.2) | collective-permute-done | bytes 262176 | tf_op jit(solution)/shard_map/ppermute | solution.py:464
  13.5 3.1 %shard_map.65 = (bf16[8,64,128]{2,1,0:T(8,128)(2,1)S(1)}, bf16[5,64,128]{2,1,0:T(8,128)(2,1)S(1)}, bf16[5,64,128]{2,1,0:T(8,128)(2,1)S(1)}) custom-call(s32[1]{0:T(128)} %bitcast.refs_0_.index, s32[4]{0:T(128)S(1)} %copy-done.2, f32[128,256]{1,0:T(8,128)S(1)} %get-tuple-element.45.acc_in, bf16[3,8,2,64,128]{4,3,2,1,0:T(8,128)(2,1)S(1)} %get-tuple-element.46.ops, ...), custom_call_target="tpu_custom_call" | custom-call | flops 671088640 | bytes 4194304 | tf_op jit(solution)/shard_map/pallas_call | solution.py:584
  16.6 0.0 collective-permute-done.refs_4_
  16.7 0.1 collective-permute-start.4
  16.7 4.7 %collective-permute-start.5 = (bf16[11,64,128]{2,1,0:T(8,128)(2,1)S(1)}, bf16[11,64,128]{2,1,0:T(8,128)(2,1)S(1)}, u32[]{:S(2)}, u32[]{:S(2)}) collective-permute-start(bf16[11,64,128]{2,1,0:T(8,128)(2,1)S(1)} %get-tuple-element.75), channel_id=1, source_target_pairs={{0,15},{1,2},{2,1},{3,4},{4,3},{5,6},{6,5},{7,8},{8,7},{9,10},{10,... | collective-permute-start | bytes 540680 | tf_op jit(solution)/shard_map/ppermute | solution.py:464
  21.5 2.1 %shard_map.66 = (f32[128,256]{1,0:T(8,128)S(1)}, bf16[3,8,2,64,128]{4,3,2,1,0:T(8,128)(2,1)S(1)}, bf16[3,8,8192]{2,1,0:T(8,128)(2,1)}) custom-call(s32[1]{0:T(128)} %bitcast.refs_0_.index, s32[4]{0:T(128)S(1)} %copy-done.2, bf16[8,64,128]{2,1,0:T(8,128)(2,1)S(1)} %get-tuple-element.52.refs_2_.refs_3_, bf16[8,64,128]{2,1,0:T(8,128)(2,1)S(1)} %slice_bitcast_fusion.refs_3_, ...), custom_call_target="tpu_custom_call" | custom-call | flops 100663296 | bytes 4194304 | tf_op jit(solution)/shard_map/pallas_call | solution.py:543
  23.6 0.0 collective-permute-done.4.one.rest_0_
  23.6 1.0 %collective-permute-done.5.two.rest_1_ = bf16[11,64,128]{2,1,0:T(8,128)(2,1)S(1)} collective-permute-done((bf16[11,64,128]{2,1,0:T(8,128)(2,1)S(1)}, bf16[11,64,128]{2,1,0:T(8,128)(2,1)S(1)}, u32[]{:S(2)}, u32[]{:S(2)}) %collective-permute-start.5) | collective-permute-done | bytes 180256 | tf_op jit(solution)/shard_map/ppermute | solution.py:464
  24.6 3.1 %shard_map.68 = (bf16[8,64,128]{2,1,0:T(8,128)(2,1)S(1)}, bf16[5,64,128]{2,1,0:T(8,128)(2,1)S(1)}, bf16[5,64,128]{2,1,0:T(8,128)(2,1)S(1)}) custom-call(s32[1]{0:T(128)} %bitcast.refs_0_.index, s32[4]{0:T(128)S(1)} %copy-done.2, f32[128,256]{1,0:T(8,128)S(1)} %get-tuple-element.55.acc_in, bf16[3,8,2,64,128]{4,3,2,1,0:T(8,128)(2,1)S(1)} %get-tuple-element.56.ops, ...), custom_call_target="tpu_custom_call" | custom-call | flops 671088640 | bytes 4194304 | tf_op jit(solution)/shard_map/pallas_call | solution.py:584
  27.8 0.0 collective-permute-done.3.refs_4_
  27.9 0.1 collective-permute-start.7
  27.9 4.5 %collective-permute-start.8 = (bf16[11,64,128]{2,1,0:T(8,128)(2,1)S(1)}, bf16[11,64,128]{2,1,0:T(8,128)(2,1)S(1)}, u32[]{:S(2)}, u32[]{:S(2)}) collective-permute-start(bf16[11,64,128]{2,1,0:T(8,128)(2,1)S(1)} %get-tuple-element.73), channel_id=1, source_target_pairs={{0,15},{1,2},{2,1},{3,4},{4,3},{5,6},{6,5},{7,8},{8,7},{9,10},{10,... | collective-permute-start | bytes 540680 | tf_op jit(solution)/shard_map/ppermute | solution.py:464
  32.4 1.5 %shard_map.69 = (f32[128,256]{1,0:T(8,128)S(1)}, bf16[3,8,2,64,128]{4,3,2,1,0:T(8,128)(2,1)S(1)}, bf16[8,8192]{1,0:T(8,128)(2,1)S(1)}) custom-call(s32[1]{0:T(128)} %bitcast.refs_0_.index, s32[4]{0:T(128)S(1)} %copy-done.2, bf16[8,64,128]{2,1,0:T(8,128)(2,1)S(1)} %get-tuple-element.62.refs_2_, bf16[8,64,128]{2,1,0:T(8,128)(2,1)S(1)} %get-tuple-element.52.refs_2_.refs_3_, ...), custom_call_target="tpu_custom_call" | custom-call | flops 100663296 | bytes 4194304 | tf_op jit(solution)/shard_map/pallas_call | solution.py:543
  34.0 0.1 collective-permute-start.6
  34.1 0.0 collective-permute-done.7.one
  34.1 1.6 %collective-permute-done.8.two = bf16[11,64,128]{2,1,0:T(8,128)(2,1)S(1)} collective-permute-done((bf16[11,64,128]{2,1,0:T(8,128)(2,1)S(1)}, bf16[11,64,128]{2,1,0:T(8,128)(2,1)S(1)}, u32[]{:S(2)}, u32[]{:S(2)}) %collective-permute-start.8) | collective-permute-done | bytes 180256 | tf_op jit(solution)/shard_map/ppermute | solution.py:464
  35.6 3.3 %shard_map.70 = bf16[8,8192]{1,0:T(8,128)(2,1)S(1)} custom-call(s32[1]{0:T(128)} %bitcast.refs_0_.index, s32[4]{0:T(128)S(1)} %copy-done.2, f32[128,256]{1,0:T(8,128)S(1)} %get-tuple-element.65.acc_in, bf16[3,8,2,64,128]{4,3,2,1,0:T(8,128)(2,1)S(1)} %get-tuple-element.66.ops, bf16[11,64,128]{2,1,0:T(8,128)(2,1)S(1)} %collective-permute-done.7.one, ...), custom_call_target="tpu_custom_call" | custom-call | flops 671088640 | bytes 4194304 | tf_op jit(solution)/shard_map/pallas_call | solution.py:584
  38.9 0.1 collective-permute-start.9
  39.0 1.9 %collective-permute-done.6 = bf16[8,8192]{1,0:T(8,128)(2,1)S(1)} collective-permute-done((bf16[8,8192]{1,0:T(8,128)(2,1)S(1)}, bf16[8,8192]{1,0:T(8,128)(2,1)S(1)}, u32[]{:S(2)}, u32[]{:S(2)}) %collective-permute-start.6) | collective-permute-done | bytes 131104 | tf_op jit(solution)/shard_map/ppermute | solution.py:464
  40.9 0.7 %bitcast_dynamic-update-slice_fusion.1 = bf16[3,8,8192]{2,1,0:T(8,128)(2,1)} fusion(bf16[3,8,8192]{2,1,0:T(8,128)(2,1)} %get-tuple-element.54, bf16[8,8192]{1,0:T(8,128)(2,1)S(1)} %collective-permute-done.6), kind=kLoop, calls=%fused_computation.9 | loop fusion | bytes 262144 | tf_op jit(solution)/shard_map/dynamic_update_slice | solution.py:648
  41.5 5.4 %collective-permute-done.9 = bf16[8,8192]{1,0:T(8,128)(2,1)S(1)} collective-permute-done((bf16[8,8192]{1,0:T(8,128)(2,1)S(1)}, bf16[8,8192]{1,0:T(8,128)(2,1)S(1)}, u32[]{:S(2)}, u32[]{:S(2)}) %collective-permute-start.9) | collective-permute-done | bytes 131104 | tf_op jit(solution)/shard_map/ppermute | solution.py:464
  47.0 0.7 %bitcast_dynamic-update-slice_fusion = bf16[3,8,8192]{2,1,0:T(8,128)(2,1)} fusion(bf16[3,8,8192]{2,1,0:T(8,128)(2,1)} %bitcast_dynamic-update-slice_fusion.1, bf16[8,8192]{1,0:T(8,128)(2,1)S(1)} %collective-permute-done.9), kind=kLoop, calls=%fused_computation.8 | loop fusion | bytes 262144 | tf_op jit(solution)/shard_map/dynamic_update_slice | solution.py:653
  (7 shorter events, 0.1 us)
Async XLA Ops:
  0.0 10.1 %copy-start.1 = (bf16[3,576,64]{1,2,0:T(8,128)(2,1)S(1)}, bf16[3,576,64]{1,2,0:T(8,128)(2,1)}, u32[]{:S(2)}) copy-start(bf16[3,576,64]{1,2,0:T(8,128)(2,1)} %param.10) | copy-start | bytes 663556
  0.0 10.1 %copy-start = (bf16[4,3,192,64]{2,3,1,0:T(8,128)(2,1)S(1)}, bf16[4,3,192,64]{2,3,1,0:T(8,128)(2,1)}, u32[]{:S(2)}) copy-start(bf16[4,3,192,64]{2,3,1,0:T(8,128)(2,1)} %param.11) | copy-start | bytes 884740
  1.3 10.8 %collective-permute-start.1 = (bf16[16,64,128]{2,1,0:T(8,128)(2,1)S(1)}, bf16[16,64,128]{2,1,0:T(8,128)(2,1)S(1)}, u32[]{:S(2)}, u32[]{:S(2)}) collective-permute-start(bf16[16,64,128]{2,1,0:T(8,128)(2,1)S(1)} %get-tuple-element.47), channel_id=1, source_target_pairs={{0,1},{1,0},{2,3},{3,2},{4,5},{5,4},{6,7},{7,6},{8,9},{9,8},{10,11... | collective-permute-start | bytes 786440 | tf_op jit(solution)/shard_map/ppermute | solution.py:464
  1.8 11.7 %collective-permute-start.2 = (bf16[16,64,128]{2,1,0:T(8,128)(2,1)S(1)}, bf16[16,64,128]{2,1,0:T(8,128)(2,1)S(1)}, u32[]{:S(2)}, u32[]{:S(2)}) collective-permute-start(bf16[16,64,128]{2,1,0:T(8,128)(2,1)S(1)} %get-tuple-element.48), channel_id=1, source_target_pairs={{0,15},{1,2},{2,1},{3,4},{4,3},{5,6},{6,5},{7,8},{8,7},{9,10},{10,... | collective-permute-start | bytes 786440 | tf_op jit(solution)/shard_map/ppermute | solution.py:464
  8.5 2.3 %copy-start.2 = (s32[4]{0:T(128)S(1)}, s32[4]{0:T(128)}, u32[]{:S(2)}) copy-start(s32[4]{0:T(128)} %clip.5) | copy-start | bytes 52
  8.5 2.3 %copy-start.3 = (s32[3,1,2]{0,2,1:T(2,128)S(1)}, s32[3,1,2]{0,2,1:T(2,128)}, u32[]{:S(2)}) copy-start(s32[3,1,2]{0,2,1:T(2,128)} %param.8) | copy-start | bytes 76
  8.5 8.1 %collective-permute-start = (bf16[9,64,128]{2,1,0:T(8,128)(2,1)S(1)}, bf16[9,64,128]{2,1,0:T(8,128)(2,1)S(1)}, u32[]{:S(2)}, u32[]{:S(2)}) collective-permute-start(bf16[9,64,128]{2,1,0:T(8,128)(2,1)S(1)} %shard_map.64), channel_id=1, source_target_pairs={{0,12},{1,13},{2,14},{3,15},{4,0},{5,1},{6,2},{7,3},{8,4},{9,5},{1... | collective-permute-start | bytes 442376 | tf_op jit(solution)/shard_map/ppermute | solution.py:464
  10.0 17.8 %collective-permute-start.3 = (bf16[9,64,128]{2,1,0:T(8,128)(2,1)S(1)}, bf16[9,64,128]{2,1,0:T(8,128)(2,1)S(1)}, u32[]{:S(2)}, u32[]{:S(2)}) collective-permute-start(bf16[9,64,128]{2,1,0:T(8,128)(2,1)S(1)} %shard_map.67), channel_id=1, source_target_pairs={{0,8},{1,9},{2,10},{3,11},{4,12},{5,13},{6,14},{7,15},{8,0},{9,1},... | collective-permute-start | bytes 442376 | tf_op jit(solution)/shard_map/ppermute | solution.py:464
  16.7 7.0 %collective-permute-start.4 = (bf16[11,64,128]{2,1,0:T(8,128)(2,1)S(1)}, bf16[11,64,128]{2,1,0:T(8,128)(2,1)S(1)}, u32[]{:S(2)}, u32[]{:S(2)}) collective-permute-start(bf16[11,64,128]{2,1,0:T(8,128)(2,1)S(1)} %get-tuple-element.76), channel_id=1, source_target_pairs={{0,1},{1,0},{2,3},{3,2},{4,5},{5,4},{6,7},{7,6},{8,9},{9,8},{10,11... | collective-permute-start | bytes 540680 | tf_op jit(solution)/shard_map/ppermute | solution.py:464
  16.7 7.9 %collective-permute-start.5 = (bf16[11,64,128]{2,1,0:T(8,128)(2,1)S(1)}, bf16[11,64,128]{2,1,0:T(8,128)(2,1)S(1)}, u32[]{:S(2)}, u32[]{:S(2)}) collective-permute-start(bf16[11,64,128]{2,1,0:T(8,128)(2,1)S(1)} %get-tuple-element.75), channel_id=1, source_target_pairs={{0,15},{1,2},{2,1},{3,4},{4,3},{5,6},{6,5},{7,8},{8,7},{9,10},{10,... | collective-permute-start | bytes 540680 | tf_op jit(solution)/shard_map/ppermute | solution.py:464
  27.9 6.2 %collective-permute-start.7 = (bf16[11,64,128]{2,1,0:T(8,128)(2,1)S(1)}, bf16[11,64,128]{2,1,0:T(8,128)(2,1)S(1)}, u32[]{:S(2)}, u32[]{:S(2)}) collective-permute-start(bf16[11,64,128]{2,1,0:T(8,128)(2,1)S(1)} %get-tuple-element.74), channel_id=1, source_target_pairs={{0,1},{1,0},{2,3},{3,2},{4,5},{5,4},{6,7},{7,6},{8,9},{9,8},{10,11... | collective-permute-start | bytes 540680 | tf_op jit(solution)/shard_map/ppermute | solution.py:464
  27.9 7.7 %collective-permute-start.8 = (bf16[11,64,128]{2,1,0:T(8,128)(2,1)S(1)}, bf16[11,64,128]{2,1,0:T(8,128)(2,1)S(1)}, u32[]{:S(2)}, u32[]{:S(2)}) collective-permute-start(bf16[11,64,128]{2,1,0:T(8,128)(2,1)S(1)} %get-tuple-element.73), channel_id=1, source_target_pairs={{0,15},{1,2},{2,1},{3,4},{4,3},{5,6},{6,5},{7,8},{8,7},{9,10},{10,... | collective-permute-start | bytes 540680 | tf_op jit(solution)/shard_map/ppermute | solution.py:464
  34.0 6.9 %collective-permute-start.6 = (bf16[8,8192]{1,0:T(8,128)(2,1)S(1)}, bf16[8,8192]{1,0:T(8,128)(2,1)S(1)}, u32[]{:S(2)}, u32[]{:S(2)}) collective-permute-start(bf16[8,8192]{1,0:T(8,128)(2,1)S(1)} %get-tuple-element.64), channel_id=1, source_target_pairs={{0,4},{1,5},{2,6},{3,7},{4,8},{5,9},{6,10},{7,11},{8,12},{9,13},{1... | collective-permute-start | bytes 393224 | tf_op jit(solution)/shard_map/ppermute | solution.py:464
  38.9 8.1 %collective-permute-start.9 = (bf16[8,8192]{1,0:T(8,128)(2,1)S(1)}, bf16[8,8192]{1,0:T(8,128)(2,1)S(1)}, u32[]{:S(2)}, u32[]{:S(2)}) collective-permute-start(bf16[8,8192]{1,0:T(8,128)(2,1)S(1)} %shard_map.70), channel_id=1, source_target_pairs={{0,8},{1,9},{2,10},{3,11},{4,12},{5,13},{6,14},{7,15},{8,0},{9,1},... | collective-permute-start | bytes 393224 | tf_op jit(solution)/shard_map/ppermute | solution.py:464
